TPU v7x, 768 devices: a whole 4x8x12 slice. The times are simulated.
768 devices in a mesh: dp: 24 (over z, core), seq: 4 (over x), head: 8 (over y).
Axes of the slice: x: 4, y: 8, z: 12, core: 2. Of those that a mesh axis runs over, the one named last changes fastest.
Arguments:
- queries: bfloat16 [24, 1440, 2048], P('dp', 'seq', 'head'), may hold values from -40 to 40
- key_rows: bfloat16 [24, 1440, 1024], P('dp', 'seq', 'head'), may hold values from -6 to 6
- value_rows: bfloat16 [24, 1440, 1024], P('dp', 'seq', 'head'), may hold values from -6 to 6
- grad_out: bfloat16 [24, 1440, 2048], P('dp', 'seq', 'head'), may hold values from -6 to 6
- doc_lengths: int32 [24, 4], P('dp'), may hold values from 2 to 1080, as said below
- dest_index: int32 [24, 1440], P('dp', 'seq'), may hold values from 0 to 23, as said below
Outputs:
- attended: bfloat16 [24, 1440, 2048], P('dp', 'seq', 'head')
- query_grad: bfloat16 [24, 1440, 2048], P('dp', 'seq', 'head')
- key_grad: bfloat16 [24, 1440, 1024], P('dp', 'seq', 'head')
- value_grad: bfloat16 [24, 1440, 1024], P('dp', 'seq', 'head')
Inputs may be any that keep to these rules, and one draw needn't show every extreme that they name: `dest_index`: within each loader sequence and each shard of 360 positions, every value 0 to 23 appears exactly 360 / 24 times. `doc_lengths`: each row holds 4 lengths that sum to 1440; the largest is exactly 1080.
All inputs are finite; a program needn't handle non-finite values.
Results may differ from a plain program's by a relative error of at most 0.0095.
Values may be sent and summed in bfloat16 or wider, within the bound.
A program may use at most 32 MiB of HBM per device.

v0:
```python
import jax
import jax.numpy as jnp
from jax import lax
from jax.sharding import PartitionSpec as P

HEAD_DIM = 128
WINDOW = 1024


score_scale = 168.0 ** (-0.5)
neg_large = -1e30


def document_ids(lengths, positions):
    boundary = jnp.cumsum(lengths, dtype=jnp.int32)
    return jnp.sum((positions[:, None] >= boundary[None, :]).astype(jnp.int32), axis=1)


def local(queries, key_rows, value_rows, grad_out, doc_lengths, dest_index):
    row_count = queries.shape[1]
    peer_count = lax.axis_size("dp")
    group_rows = row_count // peer_count
    span_count = lax.axis_size("seq")
    shard_index = lax.axis_index("seq")
    query_cols = queries.shape[2]
    key_cols = key_rows.shape[2]
    local_rows = jnp.arange(row_count, dtype=jnp.int32)
    send_order = jnp.argsort(dest_index[0] * row_count + local_rows)
    back_order = jnp.argsort(send_order)

    def outgoing(values):
        return values[0][send_order].reshape(peer_count, group_rows, values.shape[2])

    def homeward(values):
        return values.reshape(peer_count, group_rows, values.shape[1])

    def settle(values):
        return values.reshape(row_count, values.shape[2])[back_order][None]

    arrived = (
        lax.all_to_all(outgoing(queries), "dp", split_axis=0, concat_axis=0, tiled=True),
        lax.all_to_all(outgoing(key_rows), "dp", split_axis=0, concat_axis=0, tiled=True),
        lax.all_to_all(outgoing(value_rows), "dp", split_axis=0, concat_axis=0, tiled=True),
        lax.all_to_all(outgoing(grad_out), "dp", split_axis=0, concat_axis=0, tiled=True),
    )
    query_here = arrived[0].reshape(row_count, query_cols)
    key_here = arrived[1].reshape(row_count, key_cols)
    value_here = arrived[2].reshape(row_count, key_cols)
    grad_here = arrived[3].reshape(row_count, query_cols)
    reach_back = min(span_count - 1, (WINDOW + row_count - 2) // row_count)
    context_rows = (reach_back + 1) * row_count
    lead_rows = reach_back * row_count
    skip_rows = max(0, lead_rows - (WINDOW - 1))
    used_rows = context_rows - skip_rows
    full_keys, full_values = (
        lax.all_gather(key_here, "seq", axis=0, tiled=True),
        lax.all_gather(value_here, "seq", axis=0, tiled=True),
    )
    blank_rows = jnp.zeros((lead_rows, key_cols), jnp.bfloat16)
    ctx_keys = lax.dynamic_slice_in_dim(
        jnp.concatenate([blank_rows, full_keys], axis=0),
        shard_index * row_count + skip_rows,
        used_rows,
        0,
    )
    ctx_values = lax.dynamic_slice_in_dim(
        jnp.concatenate([blank_rows, full_values], axis=0),
        shard_index * row_count + skip_rows,
        used_rows,
        0,
    )
    seq_length = row_count * span_count
    all_docs = document_ids(doc_lengths[0], jnp.arange(seq_length, dtype=jnp.int32))
    padded_docs = jnp.concatenate([jnp.full((lead_rows,), -1, jnp.int32), all_docs])
    query_docs = lax.dynamic_slice_in_dim(all_docs, shard_index * row_count, row_count, 0)
    key_docs = lax.dynamic_slice_in_dim(
        padded_docs, shard_index * row_count + skip_rows, used_rows, 0
    )
    distance = (lead_rows - skip_rows + local_rows)[:, None] - jnp.arange(
        used_rows, dtype=jnp.int32
    )[None, :]
    allowed = (query_docs[:, None] == key_docs[None, :]) & (distance >= 0) & (distance < WINDOW)
    query_three = query_here.reshape(row_count, 2, HEAD_DIM)
    key_group = ctx_keys
    value_group = ctx_values
    scores = (
        jnp.einsum("qhd,kd->hqk", query_three, key_group, preferred_element_type=jnp.float32)
        * score_scale
    )
    scores = jnp.where(allowed[None], scores, neg_large)
    row_peak = jnp.max(scores, axis=2, keepdims=True)
    weights = jnp.where(allowed[None], jnp.exp(scores - row_peak), 0.0)
    prob_rows = weights / jnp.sum(weights, axis=2, keepdims=True)
    prob_low = prob_rows.astype(jnp.bfloat16)
    mixed_rows = jnp.einsum(
        "hqk,kd->qhd", prob_low, value_group, preferred_element_type=jnp.float32
    )
    head_outs = mixed_rows.astype(jnp.bfloat16).reshape(row_count, 2 * HEAD_DIM)
    saved_terms = (query_three, key_group, value_group, prob_rows, prob_low)
    query_three, key_group, value_group, prob_rows, prob_low = saved_terms
    grad_three = grad_here.reshape(row_count, 2, HEAD_DIM)
    value_parts = [
        jnp.einsum("hqk,qhd->kd", prob_low, grad_three, preferred_element_type=jnp.float32)
    ]
    prob_grad = jnp.einsum(
        "qhd,kd->hqk", grad_three, value_group, preferred_element_type=jnp.float32
    )
    center = jnp.sum(prob_rows * prob_grad, axis=2, keepdims=True)
    dscore = (prob_rows * (prob_grad - center) * score_scale).astype(jnp.bfloat16)
    query_grads = (
        jnp.einsum("hqk,kd->qhd", dscore, key_group, preferred_element_type=jnp.float32)
        .astype(jnp.bfloat16)
        .reshape(row_count, 2 * HEAD_DIM)
    )
    key_parts = [jnp.einsum("hqk,qhd->kd", dscore, query_three, preferred_element_type=jnp.float32)]
    front_zeros = jnp.zeros((skip_rows, key_cols), jnp.float32)
    key_low = lax.optimization_barrier(
        jnp.concatenate([front_zeros] + key_parts, axis=0).astype(jnp.bfloat16)
    )
    value_low = lax.optimization_barrier(
        jnp.concatenate([front_zeros] + value_parts, axis=0).astype(jnp.bfloat16)
    )
    zero_rows = jnp.zeros((lead_rows + seq_length, key_cols), jnp.float32)

    def spread(portion):
        placed = lax.dynamic_update_slice_in_dim(
            zero_rows, portion.astype(jnp.float32), shard_index * row_count, 0
        )
        return placed[lead_rows:]

    key_sum, value_sum = (
        lax.psum_scatter(
            spread(key_low).astype(jnp.bfloat16), "seq", scatter_dimension=0, tiled=True
        ).astype(jnp.float32),
        lax.psum_scatter(
            spread(value_low).astype(jnp.bfloat16), "seq", scatter_dimension=0, tiled=True
        ).astype(jnp.float32),
    )
    key_grad = key_sum.astype(jnp.bfloat16)
    value_grad = value_sum.astype(jnp.bfloat16)
    home_rows = (
        lax.all_to_all(homeward(head_outs), "dp", split_axis=0, concat_axis=0, tiled=True),
        lax.all_to_all(homeward(query_grads), "dp", split_axis=0, concat_axis=0, tiled=True),
        lax.all_to_all(homeward(key_grad), "dp", split_axis=0, concat_axis=0, tiled=True),
        lax.all_to_all(homeward(value_grad), "dp", split_axis=0, concat_axis=0, tiled=True),
    )
    return (settle(home_rows[0]), settle(home_rows[1]), settle(home_rows[2]), settle(home_rows[3]))


def solution(mesh):
    return jax.shard_map(
        local,
        mesh=mesh,
        in_specs=(
            P("dp", "seq", "head"),
            P("dp", "seq", "head"),
            P("dp", "seq", "head"),
            P("dp", "seq", "head"),
            P("dp", None),
            P("dp", "seq"),
        ),
        out_specs=(
            P("dp", "seq", "head"),
            P("dp", "seq", "head"),
            P("dp", "seq", "head"),
            P("dp", "seq", "head"),
        ),
        check_vma=False,
    )
```

profile of v0, /device:TPU:1, one launch (start us, length us, event | category | flops | bytes accessed | tf_op | source)
XLA Modules:
  0.0 224.5 jit_solution(8298137790449909336)
XLA Ops:
  7.2 0.7 multiply_reduce_fusion
  8.0 3.8 %sort.31 = (s32[360]{0:T(512)}, s32[360]{0:T(512)S(1)}) sort(s32[360]{0:T(512)S(1)} %iota_add_fusion.1, s32[360]{0:T(512)S(1)} %iota.29), dimensions={0}, to_apply=%region_0.0 | sort | flops 3240 | bytes 5760 | tf_op jit(solution)/shard_map/jit(argsort)/sort | solution.py:28
  11.7 2.1 gather_fusion
  13.8 0.7 reshape.127
  14.5 16.7 %all-to-all-start = ((bf16[24,15,128]{2,1,0:T(8,128)(2,1)}), bf16[24,15,128]{2,1,0:T(8,128)(2,1)S(1)}, u32[]{:S(2)}, u32[]{:S(2)}) async-start(bf16[24,15,128]{2,1,0:T(8,128)(2,1)} %reshape.127), calls=%async_computation | async-start | bytes 196608 | tf_op jit(solution)/shard_map/all_to_all | solution.py:43
  31.2 2.1 gather_fusion.1
  33.3 0.7 reshape.131
  34.0 0.8 reduce-window.8
  34.8 7.5 %all-to-all-done = bf16[24,15,128]{2,1,0:T(8,128)(2,1)S(1)} async-done(((bf16[24,15,128]{2,1,0:T(8,128)(2,1)}), bf16[24,15,128]{2,1,0:T(8,128)(2,1)S(1)}, u32[]{:S(2)}, u32[]{:S(2)}) %all-to-all-start) | async-done | bytes 92192 | tf_op jit(solution)/shard_map/all_to_all | solution.py:43
  42.3 4.2 %all-to-all-start.1 = ((bf16[24,15,128]{2,1,0:T(8,128)(2,1)}), bf16[24,15,128]{2,1,0:T(8,128)(2,1)S(1)}, u32[]{:S(2)}, u32[]{:S(2)}) async-start(bf16[24,15,128]{2,1,0:T(8,128)(2,1)} %reshape.131), calls=%async_computation.1 | async-start | bytes 196608 | tf_op jit(solution)/shard_map/all_to_all | solution.py:42
  46.6 2.0 gather_fusion.2
  48.6 0.7 reshape.133
  49.4 2.0 gather_fusion.4
  51.4 0.7 reshape.135
  52.3 5.3 %all-to-all-done.1 = bf16[24,15,128]{2,1,0:T(8,128)(2,1)S(1)} async-done(((bf16[24,15,128]{2,1,0:T(8,128)(2,1)}), bf16[24,15,128]{2,1,0:T(8,128)(2,1)S(1)}, u32[]{:S(2)}, u32[]{:S(2)}) %all-to-all-start.1) | async-done | bytes 92192 | tf_op jit(solution)/shard_map/all_to_all | solution.py:42
  57.6 4.5 %all-to-all-start.2 = ((bf16[24,15,256]{2,1,0:T(8,128)(2,1)}), bf16[24,15,256]{2,1,0:T(8,128)(2,1)S(1)}, u32[]{:S(2)}, u32[]{:S(2)}) async-start(bf16[24,15,256]{2,1,0:T(8,128)(2,1)} %reshape.133), calls=%async_computation.2 | async-start | bytes 393216 | tf_op jit(solution)/shard_map/all_to_all | solution.py:41
  62.1 0.8 fusion.11
  63.0 10.8 %all_gather.6 = bf16[1440,128]{1,0:T(8,128)(2,1)S(1)} all-gather(bf16[360,128]{1,0:T(8,128)(2,1)S(1)} %reshape.128), channel_id=1, replica_groups=mesh['dp'=24,'seq'=4,'head'=8] {'seq'}, dimensions={0}, use_global_device_ids=true | all-gather | bytes 460800 | tf_op jit(solution)/shard_map/all_gather | solution.py:57
  73.8 9.6 %all_gather.7 = bf16[1440,128]{1,0:T(8,128)(2,1)S(1)} all-gather(bf16[360,128]{1,0:T(8,128)(2,1)S(1)} %reshape.132), channel_id=1, replica_groups=mesh['dp'=24,'seq'=4,'head'=8] {'seq'}, dimensions={0}, use_global_device_ids=true | all-gather | bytes 460800 | tf_op jit(solution)/shard_map/all_gather | solution.py:56
  83.4 14.9 %all-to-all-start.4 = ((bf16[24,15,256]{2,1,0:T(8,128)(2,1)}), bf16[24,15,256]{2,1,0:T(8,128)(2,1)S(1)}, u32[]{:S(2)}, u32[]{:S(2)}) async-start(bf16[24,15,256]{2,1,0:T(8,128)(2,1)} %reshape.135), calls=%async_computation.4 | async-start | bytes 393216 | tf_op jit(solution)/shard_map/all_to_all | solution.py:44
  98.4 4.4 %fusion.57 = (f32[2,360]{1,0:T(2,128)S(1)}, f32[2,360,1383]{2,1,0:T(8,128)}) fusion(pred[360,1383]{1,0:T(8,128)(4,1)S(1)} %fusion.11, s32[]{:T(128)S(6)} %select_n.32, bf16[1440,128]{1,0:T(8,128)(2,1)S(1)} %all_gather.7, bf16[360,2,128]{2,1,0:T(2,128)(2,1)S(1)} %reshape_reshape.12), kind=kOutput, calls=%fused_computation.77 | convolution fusion | flops 259894736 | bytes 5552644 | tf_op jit(solution)/shard_map/sub | solution.py:92
  102.7 3.2 %fusion.16 = bf16[360,2,128]{2,0,1:T(8,128)(2,1)S(1)} fusion(s32[]{:T(128)S(6)} %select_n.32, bf16[1440,128]{1,0:T(8,128)(2,1)S(1)} %all_gather.6, f32[2,360,1383]{2,1,0:T(8,128)} %get-tuple-element.9, f32[2,360]{1,0:T(2,128)S(1)} %get-tuple-element.8), kind=kOutput, calls=%fused_computation.33 | convolution fusion | flops 256998240 | bytes 4538884 | tf_op jit(solution)/shard_map/hqk,kd->qhd/dot_general | solution.py:95
  106.1 0.8 reshape_reshape.13
  106.9 5.1 %all-to-all-done.4 = bf16[24,15,256]{2,1,0:T(8,128)(2,1)S(1)} async-done(((bf16[24,15,256]{2,1,0:T(8,128)(2,1)}), bf16[24,15,256]{2,1,0:T(8,128)(2,1)S(1)}, u32[]{:S(2)}, u32[]{:S(2)}) %all-to-all-start.4) | async-done | bytes 184352 | tf_op jit(solution)/shard_map/all_to_all | solution.py:44
  112.0 4.6 %all-to-all-start.3 = ((bf16[24,15,256]{2,1,0:T(8,128)(2,1)}), bf16[24,15,256]{2,1,0:T(8,128)(2,1)S(1)}, u32[]{:S(2)}, u32[]{:S(2)}) async-start(bf16[24,15,256]{2,1,0:T(8,128)(2,1)} %reshape_reshape.13), calls=%async_computation.3 | async-start | bytes 393216 | tf_op jit(solution)/shard_map/all_to_all | solution.py:142
  116.6 0.2 reduce-scatter.7.cloned.1.call-start
  116.9 3.1 %fusion.23 = f32[1383,360,2]{0,1,2:T(8,128)} fusion(s32[]{:T(128)S(6)} %select_n.32, bf16[1440,128]{1,0:T(8,128)(2,1)S(1)} %all_gather.6, bf16[360,2,128]{2,1,0:T(2,128)(2,1)S(1)} %reshape_reshape.14), kind=kOutput, calls=%fused_computation.44 | convolution fusion | flops 254914560 | bytes 4536004 | tf_op jit(solution)/shard_map/qhd,kd->hqk/dot_general | solution.py:105
  119.9 10.5 %fusion.6 = bf16[1383,128]{1,0:T(8,128)(2,1)S(1)} fusion(f32[1383,360,2]{0,1,2:T(8,128)} %fusion.23, bf16[360,2,128]{2,1,0:T(2,128)(2,1)S(1)} %reshape_reshape.12, f32[2,360,1383]{2,1,0:T(8,128)} %get-tuple-element.9, f32[2,360]{1,0:T(2,128)S(1)} %get-tuple-element.8), kind=kOutput, calls=%fused_computation.20 | convolution fusion | flops 262064000 | bytes 8507328 | tf_op jit(solution)/shard_map/hqk,qhd->kd/dot_general | solution.py:115
  130.7 0.8 slice.31
  131.5 3.1 %fusion.7 = bf16[1383,128]{1,0:T(8,128)(2,1)S(1)} fusion(bf16[360,2,128]{2,1,0:T(2,128)(2,1)S(1)} %reshape_reshape.14, f32[2,360,1383]{2,1,0:T(8,128)} %get-tuple-element.9, f32[2,360]{1,0:T(2,128)S(1)} %get-tuple-element.8), kind=kOutput, calls=%fused_computation.21 | convolution fusion | flops 257083104 | bytes 4524288 | tf_op jit(solution)/shard_map/hqk,qhd->kd/dot_general | solution.py:103
  134.6 9.0 %fusion.15 = bf16[360,2,128]{2,0,1:T(8,128)(2,1)S(1)} fusion(f32[1383,360,2]{0,1,2:T(8,128)} %fusion.23, s32[]{:T(128)S(6)} %select_n.32, bf16[1440,128]{1,0:T(8,128)(2,1)S(1)} %all_gather.7, f32[2,360,1383]{2,1,0:T(8,128)} %get-tuple-element.9, f32[2,360]{1,0:T(2,128)S(1)} %get-tuple-element.8), kind=kOutput, calls=%fused_computation.32 | convolution fusion | flops 261979136 | bytes 16779268 | tf_op jit(solution)/shard_map/hqk,kd->qhd/dot_general | solution.py:111
  143.6 0.1 copy.25
  143.8 0.8 reshape_reshape.15
  144.7 9.8 %all-to-all-start.5 = ((bf16[24,15,256]{2,1,0:T(8,128)(2,1)}), bf16[24,15,256]{2,1,0:T(8,128)(2,1)S(1)}, u32[]{:S(2)}, u32[]{:S(2)}) async-start(bf16[24,15,256]{2,1,0:T(8,128)(2,1)} %reshape_reshape.15), calls=%async_computation.5 | async-start | bytes 393216 | tf_op jit(solution)/shard_map/all_to_all | solution.py:143
  154.7 0.8 slice.30
  155.4 2.8 %reduce-scatter.7.cloned.1.call-done = bf16[360,128]{1,0:T(8,128)(2,1)} async-done(((bf16[1440,128]{1,0:T(8,128)(2,1)}), bf16[360,128]{1,0:T(8,128)(2,1)}) %reduce-scatter.7.cloned.1.call-update) | async-done | bytes 92176
  158.3 1.6 reshape.137
  159.9 8.3 %all-to-all-done.5 = bf16[24,15,256]{2,1,0:T(8,128)(2,1)S(1)} async-done(((bf16[24,15,256]{2,1,0:T(8,128)(2,1)}), bf16[24,15,256]{2,1,0:T(8,128)(2,1)S(1)}, u32[]{:S(2)}, u32[]{:S(2)}) %all-to-all-start.5) | async-done | bytes 184352 | tf_op jit(solution)/shard_map/all_to_all | solution.py:143
  168.2 4.5 %all-to-all-start.6 = ((bf16[24,15,128]{2,1,0:T(8,128)(2,1)}), bf16[24,15,128]{2,1,0:T(8,128)(2,1)S(1)}, u32[]{:S(2)}, u32[]{:S(2)}) async-start(bf16[24,15,128]{2,1,0:T(8,128)(2,1)} %reshape.137), calls=%async_computation.6 | async-start | bytes 196608 | tf_op jit(solution)/shard_map/all_to_all | solution.py:144
  172.7 3.8 %sort.32 = (s32[360]{0:T(512)}, s32[360]{0:T(512)S(1)}) sort(s32[360]{0:T(512)S(1)} %get-tuple-element.6, s32[360]{0:T(512)S(1)} %iota.31), dimensions={0}, to_apply=%region_5.6 | sort | flops 3240 | bytes 5760 | tf_op jit(solution)/shard_map/jit(argsort)/sort | solution.py:29
  176.5 13.8 %reduce-scatter.9.cloned.1.call-done = bf16[360,128]{1,0:T(8,128)(2,1)} async-done(((bf16[1440,128]{1,0:T(8,128)(2,1)}), bf16[360,128]{1,0:T(8,128)(2,1)}) %reduce-scatter.9.cloned.1.call-update) | async-done | bytes 92176
  190.3 1.6 reshape.139
  191.9 12.8 %all-to-all-start.7 = ((bf16[24,15,128]{2,1,0:T(8,128)(2,1)}), bf16[24,15,128]{2,1,0:T(8,128)(2,1)S(1)}, u32[]{:S(2)}, u32[]{:S(2)}) async-start(bf16[24,15,128]{2,1,0:T(8,128)(2,1)} %reshape.139), calls=%async_computation.7 | async-start | bytes 196608 | tf_op jit(solution)/shard_map/all_to_all | solution.py:145
  204.8 2.5 %gather_fusion.3 = bf16[360,256]{1,0:T(8,128)(2,1)} fusion(bf16[360,256]{1,0:T(8,128)(2,1)S(1)} %reshape.134, s32[1024]{0:T(1024)S(1)} %pad_clamp_fusion), kind=kCustom, calls=%fused_computation.3 | custom fusion | bytes 370080 | tf_op jit(solution)/shard_map/gather | solution.py:38
  207.4 2.5 %gather_fusion.5 = bf16[360,256]{1,0:T(8,128)(2,1)} fusion(bf16[360,256]{1,0:T(8,128)(2,1)S(1)} %reshape.136, s32[1024]{0:T(1024)S(1)} %pad_clamp_fusion), kind=kCustom, calls=%fused_computation.5 | custom fusion | bytes 370080 | tf_op jit(solution)/shard_map/gather | solution.py:38
  210.0 1.9 gather_fusion.6
  211.9 3.8 %all-to-all-done.7 = bf16[24,15,128]{2,1,0:T(8,128)(2,1)S(1)} async-done(((bf16[24,15,128]{2,1,0:T(8,128)(2,1)}), bf16[24,15,128]{2,1,0:T(8,128)(2,1)S(1)}, u32[]{:S(2)}, u32[]{:S(2)}) %all-to-all-start.7) | async-done | bytes 92192 | tf_op jit(solution)/shard_map/all_to_all | solution.py:145
  215.8 1.9 gather_fusion.7
  (36 shorter events, 1.5 us)
Async XLA Ops:
  7.2 39.4 %copy-start = (bf16[1,360,256]{2,1,0:T(8,128)(2,1)S(1)}, bf16[1,360,256]{2,1,0:T(8,128)(2,1)}, u32[]{:S(2)}) copy-start(bf16[1,360,256]{2,1,0:T(8,128)(2,1)} %param.6) | copy-start | bytes 552964
  7.2 42.2 %copy-start.1 = (bf16[1,360,256]{2,1,0:T(8,128)(2,1)S(1)}, bf16[1,360,256]{2,1,0:T(8,128)(2,1)}, u32[]{:S(2)}) copy-start(bf16[1,360,256]{2,1,0:T(8,128)(2,1)} %param.9) | copy-start | bytes 552964
  14.5 27.8 %all-to-all-start = ((bf16[24,15,128]{2,1,0:T(8,128)(2,1)}), bf16[24,15,128]{2,1,0:T(8,128)(2,1)S(1)}, u32[]{:S(2)}, u32[]{:S(2)}) async-start(bf16[24,15,128]{2,1,0:T(8,128)(2,1)} %reshape.127), calls=%async_computation | async-start | bytes 196608 | tf_op jit(solution)/shard_map/all_to_all | solution.py:43
  42.3 15.3 %all-to-all-start.1 = ((bf16[24,15,128]{2,1,0:T(8,128)(2,1)}), bf16[24,15,128]{2,1,0:T(8,128)(2,1)S(1)}, u32[]{:S(2)}, u32[]{:S(2)}) async-start(bf16[24,15,128]{2,1,0:T(8,128)(2,1)} %reshape.131), calls=%async_computation.1 | async-start | bytes 196608 | tf_op jit(solution)/shard_map/all_to_all | solution.py:42
  57.6 25.8 %all-to-all-start.2 = ((bf16[24,15,256]{2,1,0:T(8,128)(2,1)}), bf16[24,15,256]{2,1,0:T(8,128)(2,1)S(1)}, u32[]{:S(2)}, u32[]{:S(2)}) async-start(bf16[24,15,256]{2,1,0:T(8,128)(2,1)} %reshape.133), calls=%async_computation.2 | async-start | bytes 393216 | tf_op jit(solution)/shard_map/all_to_all | solution.py:41
  83.4 28.6 %all-to-all-start.4 = ((bf16[24,15,256]{2,1,0:T(8,128)(2,1)}), bf16[24,15,256]{2,1,0:T(8,128)(2,1)S(1)}, u32[]{:S(2)}, u32[]{:S(2)}) async-start(bf16[24,15,256]{2,1,0:T(8,128)(2,1)} %reshape.135), calls=%async_computation.4 | async-start | bytes 393216 | tf_op jit(solution)/shard_map/all_to_all | solution.py:44
  112.0 32.7 %all-to-all-start.3 = ((bf16[24,15,256]{2,1,0:T(8,128)(2,1)}), bf16[24,15,256]{2,1,0:T(8,128)(2,1)S(1)}, u32[]{:S(2)}, u32[]{:S(2)}) async-start(bf16[24,15,256]{2,1,0:T(8,128)(2,1)} %reshape_reshape.13), calls=%async_computation.3 | async-start | bytes 393216 | tf_op jit(solution)/shard_map/all_to_all | solution.py:142
  116.6 41.7 %reduce-scatter.7.cloned.1.call-start = ((), (), s32[]{:S(2)}) async-start(), calls=%async_computation.10 | async-start | bytes 460800
  144.7 23.5 %all-to-all-start.5 = ((bf16[24,15,256]{2,1,0:T(8,128)(2,1)}), bf16[24,15,256]{2,1,0:T(8,128)(2,1)S(1)}, u32[]{:S(2)}, u32[]{:S(2)}) async-start(bf16[24,15,256]{2,1,0:T(8,128)(2,1)} %reshape_reshape.15), calls=%async_computation.5 | async-start | bytes 393216 | tf_op jit(solution)/shard_map/all_to_all | solution.py:143
  154.5 35.9 %reduce-scatter.9.cloned.1.call-start = ((), (), s32[]{:S(2)}) async-start(), calls=%async_computation.11 | async-start | bytes 460800
  168.2 23.7 %all-to-all-start.6 = ((bf16[24,15,128]{2,1,0:T(8,128)(2,1)}), bf16[24,15,128]{2,1,0:T(8,128)(2,1)S(1)}, u32[]{:S(2)}, u32[]{:S(2)}) async-start(bf16[24,15,128]{2,1,0:T(8,128)(2,1)} %reshape.137), calls=%async_computation.6 | async-start | bytes 196608 | tf_op jit(solution)/shard_map/all_to_all | solution.py:144
  191.9 23.8 %all-to-all-start.7 = ((bf16[24,15,128]{2,1,0:T(8,128)(2,1)}), bf16[24,15,128]{2,1,0:T(8,128)(2,1)S(1)}, u32[]{:S(2)}, u32[]{:S(2)}) async-start(bf16[24,15,128]{2,1,0:T(8,128)(2,1)} %reshape.139), calls=%async_computation.7 | async-start | bytes 196608 | tf_op jit(solution)/shard_map/all_to_all | solution.py:145
Sparse Core Ops, SparseCore 0:
  131.6 26.6 reduce-scatter.6
  161.7 28.5 reduce-scatter.8
where the time goes:
time: 225 us
  starting transfers between devices  72.1 us (32%)
  waiting for transfers between devices  46.7 us (21%)
  matrix products  33.2 us (15%)
  local copies, waits for them, and re-layouts  27.5 us (12%)
  blocking collectives  20.4 us (9%)
  between operations  14.4 us (6%)
  other arithmetic  10.2 us (5%)
    unnamed x4, waiting for transfers between devices  16.7 us
    all_to_all x1, starting transfers between devices, local(): lax.all_to_all(outgoing(value_rows), 'dp', split_axis=0, concat_axis=0, t...  16.7 us
    all_to_all x1, starting transfers between devices, local(): lax.all_to_all(outgoing(grad_out), 'dp', split_axis=0, concat_axis=0, til...  14.9 us
    all_to_all x1, starting transfers between devices, local(): lax.all_to_all(homeward(value_grad), 'dp', split_axis=0, concat_axis=0, t...  12.8 us
    all_gather x1, blocking collectives, local(): lax.all_gather(value_here, 'seq', axis=0, tiled=True)  10.8 us
    dot_general x1, matrix products, local(): jnp.einsum('hqk,qhd->kd', dscore, query_three, preferred_element_type=jnp...  10.5 us
    all_to_all x1, starting transfers between devices, local(): lax.all_to_all(homeward(query_grads), 'dp', split_axis=0, concat_axis=0,...  9.75 us
    all_gather x1, blocking collectives, local(): lax.all_gather(key_here, 'seq', axis=0, tiled=True)  9.58 us
  transfers between devices with their start and end apart: 10, of which 7 were waited for; matrix products, arithmetic and copies ran while one was open for 27% of the time, Pallas kernels for 0%

commit v1 on v0

v1 whole, which is shorter than its diff:
```python
import functools
import math

import jax
import jax.numpy as jnp
from jax import lax
from jax.experimental import pallas as pl
from jax.experimental.pallas import tpu as pltpu
from jax.sharding import PartitionSpec as P

HEAD = 128
PAIR = 2 * HEAD
PAD = 16
WINDOW = 1024
DOCS = 4
SCALE = 168.0 ** (-0.5)
LOG2E = 1.0 / math.log(2.0)
NEG = -1e30
MESH = pl.DeviceIdType.MESH
BF16 = jnp.bfloat16
F32 = jnp.float32


def dot(a, b):
    return jnp.dot(a, b, preferred_element_type=F32)


def dot_nt(a, b):
    return lax.dot_general(a, b, (((1,), (1,)), ((), ())), preferred_element_type=F32)


def kernel(peers, spans, rows, window, *refs):
    (q_ref, k_ref, v_ref, dy_ref, len_ref, dest_ref, o_ref, dq_ref, dk_ref, dv_ref,
     xin, perm, unperm, sends, ctx, ctxt, recvs, homes, backs, gsend, grecv, acc,
     sbuf, dbuf, keyf, queryf, insem, ssem, rsem, xssem, xrsem) = refs
    me = lax.axis_index("dp")
    shard = lax.axis_index("seq")
    group = rows // peers
    padded = peers * PAD

    tail = padded - PAD * ((padded - rows + PAD - 1) // PAD)
    xin[pl.ds(tail, padded - tail), :] = jnp.zeros((padded - tail, 6 * HEAD), BF16)
    def fetch(ref, first, count, at, slot):
        return pltpu.make_async_copy(
            ref.at[0, :, pl.ds(first, count)],
            xin.at[pl.ds(0, rows), pl.ds(at, count)],
            insem.at[slot],
        )
    loads = [
        fetch(k_ref, 0, HEAD, 0, 0),
        fetch(v_ref, 0, HEAD, HEAD, 1),
        fetch(q_ref, 0, HEAD, 2 * HEAD, 2),
        fetch(dy_ref, 0, HEAD, 3 * HEAD, 3),
        fetch(q_ref, HEAD, HEAD, 4 * HEAD, 4),
        fetch(dy_ref, HEAD, HEAD, 5 * HEAD, 5),
    ]
    for load in loads:
        load.start()

    barrier = pltpu.get_barrier_semaphore()

    def greet(step, carry):
        pl.semaphore_signal(
            barrier, inc=1, device_id={"dp": lax.rem(me + step, peers)}, device_id_type=MESH
        )
        return carry

    lax.fori_loop(1, peers, greet, 0)
    for step in range(1, spans):
        pl.semaphore_signal(
            barrier, inc=1, device_id={"seq": lax.rem(shard + step, spans)}, device_id_type=MESH
        )

    dest = dest_ref[...]
    is_dest = (lax.broadcasted_iota(jnp.int32, (peers, rows), 0) == dest).astype(F32)
    before = (
        lax.broadcasted_iota(jnp.int32, (rows, rows), 0)
        < lax.broadcasted_iota(jnp.int32, (rows, rows), 1)
    ).astype(F32)
    counts = dot(is_dest.astype(BF16), before.astype(BF16))
    rank = jnp.sum(is_dest * counts, axis=0, keepdims=True)
    place = dest.astype(F32) * PAD + rank
    hot = (
        lax.broadcasted_iota(jnp.int32, (padded, rows), 0).astype(F32) == place
    ).astype(F32)
    perm[...] = jnp.zeros((padded, padded), F32)
    perm[:, pl.ds(0, rows)] = hot
    perm_low = perm[...].astype(BF16)

    def exchange(phase, src, dst):
        def one(step, carry):
            odd = lax.rem(step, 2)
            far = peers // 2 - (step + 1) // 2
            ahead = (1 - odd) * far + odd * (peers - far)
            peer = lax.rem(me + ahead, peers)
            pltpu.make_async_remote_copy(
                src_ref=src.at[pl.ds(pl.multiple_of(peer * PAD, PAD), PAD)],
                dst_ref=dst.at[pl.ds(pl.multiple_of(me * PAD, PAD), PAD)],
                send_sem=ssem.at[phase],
                recv_sem=rsem.at[phase],
                device_id={"dp": peer},
                device_id_type=MESH,
            ).start()
            return carry

        lax.fori_loop(0, peers - 1, one, 0)
        own = pl.ds(pl.multiple_of(me * PAD, PAD), PAD)
        pltpu.make_async_copy(src.at[own], dst.at[own], rsem.at[phase]).start()

    def arrived(phase, dst):
        pltpu.make_async_copy(dst, dst, rsem.at[phase]).wait()

    def departed(phase, src):
        sent = src.at[pl.ds(0, padded - PAD)]
        pltpu.make_async_copy(sent, sent, ssem.at[phase]).wait()

    landing = (ctx.at[pl.ds(0, padded)], recvs.at[0], recvs.at[1])
    for phase in range(3):
        loads[2 * phase].wait()
        loads[2 * phase + 1].wait()
        sends[phase] = dot(perm_low, xin[:, pl.ds(phase * PAIR, PAIR)]).astype(BF16)
        if phase == 0:
            pl.semaphore_wait(barrier, peers - 1 + spans - 1)
        exchange(phase, sends.at[phase], landing[phase])

    unperm[...] = perm[...].T.astype(BF16)
    bounds = [len_ref[0, 0]]
    for entry in range(1, DOCS):
        bounds.append(bounds[-1] + len_ref[0, entry])

    slot_row = lax.broadcasted_iota(jnp.int32, (padded, HEAD), 0)
    column = lax.broadcasted_iota(jnp.int32, (padded, HEAD), 1)
    local = (slot_row // PAD) * group + lax.rem(slot_row, PAD)
    blank = lax.rem(slot_row, PAD) >= group

    def documents(position):
        total = jnp.zeros_like(position)
        for bound in bounds:
            total = total + (position >= bound).astype(jnp.int32)
        return total

    queryf[...] = (documents(local + shard * rows) == column).astype(F32).astype(BF16)
    for back in range(spans):
        position = local + (shard - back) * rows
        shut = (documents(position) != column) | blank | (position < 0)
        keyf[pl.ds(back * padded, padded)] = jnp.where(
            shut & (column <= DOCS), NEG, 0.0
        ).astype(BF16)
    for back in range(1, spans):
        @pl.when(shard < back)
        def _():
            ctx[pl.ds(back * padded, padded)] = jnp.zeros((padded, PAIR), BF16)

    arrived(0, landing[0])

    def forward(back):
        return pltpu.make_async_remote_copy(
            src_ref=ctx.at[pl.ds(0, padded)],
            dst_ref=ctx.at[pl.ds(back * padded, padded)],
            send_sem=xssem.at[back],
            recv_sem=xrsem.at[back],
            device_id={"seq": lax.rem(shard + back, spans)},
            device_id_type=MESH,
        )

    for back in range(1, spans):
        @pl.when(shard + back < spans)
        def _():
            forward(back).start()
    for back in range(1, spans):
        @pl.when(shard >= back)
        def _():
            forward(back).wait_recv()
    for back in range(spans):
        block = pl.ds(back * padded, padded)
        ctxt[:, block] = ctx[block, :].astype(F32).T.astype(BF16)

    key_row = lax.broadcasted_iota(jnp.int32, (padded, padded), 0)
    query_col = lax.broadcasted_iota(jnp.int32, (padded, padded), 1)

    def spot(index):
        return (index // PAD) * group + lax.rem(index, PAD)

    def attend(member):
        arrived(1 + member, landing[1 + member])
        query = recvs[member, :, pl.ds(0, HEAD)]
        grad = recvs[member, :, pl.ds(HEAD, HEAD)]
        query_wide = jnp.concatenate([query, queryf[...]], axis=1)
        peak = None
        for back in range(spans):
            block = pl.ds(back * padded, padded)
            key_wide = jnp.concatenate([ctx[block, pl.ds(0, HEAD)], keyf[block, :]], axis=1)
            scores = dot_nt(key_wide, query_wide)
            if back == 0:
                scores = jnp.where(query_col >= key_row, scores, NEG)
            if back * rows + rows - 1 >= window:
                gap = back * rows + spot(query_col) - spot(key_row)
                scores = jnp.where(gap < window, scores, NEG)
            sbuf[block, :] = scores
            top = jnp.max(scores, axis=0, keepdims=True)
            peak = top if peak is None else jnp.maximum(peak, top)
        total = jnp.zeros((1, padded), F32)
        for back in range(spans):
            block = pl.ds(back * padded, padded)
            weight = jnp.exp2((sbuf[block, :] - peak) * (SCALE * LOG2E))
            sbuf[block, :] = weight
            total = total + jnp.sum(weight, axis=0, keepdims=True)
        share = 1.0 / total
        mixed = jnp.zeros((HEAD, padded), F32)
        center = jnp.zeros((1, padded), F32)
        for back in range(spans):
            block = pl.ds(back * padded, padded)
            prob = sbuf[block, :] * share
            sbuf[block, :] = prob
            low = prob.astype(BF16)
            dprob = dot_nt(ctx[block, pl.ds(HEAD, HEAD)], grad)
            dbuf[block, :] = dprob
            center = center + jnp.sum(prob * dprob, axis=0, keepdims=True)
            mixed = mixed + dot(ctxt[pl.ds(HEAD, HEAD), block], low)
            part = dot(low, grad)
            if member == 0:
                acc[block, pl.ds(HEAD, HEAD)] = part
            else:
                acc[block, pl.ds(HEAD, HEAD)] += part
        dquery = jnp.zeros((HEAD, padded), F32)
        for back in range(spans):
            block = pl.ds(back * padded, padded)
            dscore = (sbuf[block, :] * (dbuf[block, :] - center)).astype(BF16)
            dquery = dquery + dot(ctxt[pl.ds(0, HEAD), block], dscore)
            part = dot(dscore, query) * SCALE
            if member == 0:
                acc[block, pl.ds(0, HEAD)] = part
            else:
                acc[block, pl.ds(0, HEAD)] += part
        homes[member, :, pl.ds(0, HEAD)] = mixed.T.astype(BF16)
        homes[member, :, pl.ds(HEAD, HEAD)] = (dquery * SCALE).T.astype(BF16)
        exchange(3 + member, homes.at[member], backs.at[member])

    attend(0)
    attend(1)

    def give(back):
        return pltpu.make_async_remote_copy(
            src_ref=gsend.at[back],
            dst_ref=grecv.at[back],
            send_sem=xssem.at[spans + back],
            recv_sem=xrsem.at[spans + back],
            device_id={"seq": lax.rem(shard + spans - back, spans)},
            device_id_type=MESH,
        )

    for back in range(spans - 1, -1, -1):
        gsend[back] = acc[pl.ds(back * padded, padded), :].astype(BF16)
        if back > 0:
            @pl.when(shard >= back)
            def _():
                give(back).start()
    acc[pl.ds(0, padded), :] = gsend[0].astype(F32)
    for back in range(1, spans):
        @pl.when(shard + back < spans)
        def _():
            give(back).wait_recv()
            acc[pl.ds(0, padded), :] += grecv[back].astype(F32)
    homes[2] = acc[pl.ds(0, padded), :].astype(BF16)
    exchange(5, homes.at[2], backs.at[2])

    def settle(member):
        arrived(3 + member, backs.at[member])
        return dot(unperm[...], backs[member]).astype(BF16)

    for member in range(2):
        rows_home = settle(member)
        o_ref[0, :, pl.ds(member * HEAD, HEAD)] = rows_home[:rows, :HEAD]
        dq_ref[0, :, pl.ds(member * HEAD, HEAD)] = rows_home[:rows, HEAD:]
    rows_home = settle(2)
    dk_ref[0] = rows_home[:rows, :HEAD]
    dv_ref[0] = rows_home[:rows, HEAD:]

    for phase in range(3):
        departed(phase, sends.at[phase])
        departed(3 + phase, homes.at[phase])
    for back in range(1, spans):
        @pl.when(shard + back < spans)
        def _():
            forward(back).wait_send()
        @pl.when(shard >= back)
        def _():
            give(back).wait_send()


def solution(mesh, window=WINDOW):
    peers, spans = mesh.shape["dp"], mesh.shape["seq"]

    def local(queries, key_rows, value_rows, grad_out, doc_lengths, dest_index):
        rows = queries.shape[1]
        padded = peers * PAD
        blocks = spans * padded
        whole = pl.BlockSpec(memory_space=pltpu.VMEM)
        loose = pl.BlockSpec(memory_space=pl.ANY)
        return pl.pallas_call(
            functools.partial(kernel, peers, spans, rows, window),
            out_shape=(
                jax.ShapeDtypeStruct((1, rows, PAIR), BF16),
                jax.ShapeDtypeStruct((1, rows, PAIR), BF16),
                jax.ShapeDtypeStruct((1, rows, HEAD), BF16),
                jax.ShapeDtypeStruct((1, rows, HEAD), BF16),
            ),
            in_specs=[loose] * 4 + [pl.BlockSpec(memory_space=pltpu.SMEM), whole],
            out_specs=(whole,) * 4,
            scratch_shapes=[
                pltpu.VMEM((padded, 6 * HEAD), BF16),
                pltpu.VMEM((padded, padded), F32),
                pltpu.VMEM((padded, padded), BF16),
                pltpu.VMEM((3, padded, PAIR), BF16),
                pltpu.VMEM((blocks, PAIR), BF16),
                pltpu.VMEM((PAIR, blocks), BF16),
                pltpu.VMEM((2, padded, PAIR), BF16),
                pltpu.VMEM((3, padded, PAIR), BF16),
                pltpu.VMEM((3, padded, PAIR), BF16),
                pltpu.VMEM((spans, padded, PAIR), BF16),
                pltpu.VMEM((spans, padded, PAIR), BF16),
                pltpu.VMEM((blocks, PAIR), F32),
                pltpu.VMEM((blocks, padded), F32),
                pltpu.VMEM((blocks, padded), F32),
                pltpu.VMEM((blocks, HEAD), BF16),
                pltpu.VMEM((padded, HEAD), BF16),
                pltpu.SemaphoreType.DMA((6,)),
                pltpu.SemaphoreType.DMA((6,)),
                pltpu.SemaphoreType.DMA((6,)),
                pltpu.SemaphoreType.DMA((2 * spans,)),
                pltpu.SemaphoreType.DMA((2 * spans,)),
            ],
            compiler_params=pltpu.CompilerParams(
                collective_id=0, has_side_effects=True, vmem_limit_bytes=40 << 20
            ),
        )(queries, key_rows, value_rows, grad_out, doc_lengths, dest_index)

    wide = P("dp", "seq", "head")
    return jax.shard_map(
        local,
        mesh=mesh,
        in_specs=(wide, wide, wide, wide, P("dp", None), P("dp", "seq")),
        out_specs=(wide, wide, wide, wide),
        check_vma=False,
    )
```

time: 225 us -> 73.7 us (0.33)
  starting transfers between devices: 72.1 us -> 0 us
  Pallas kernels: 0 us -> 65.2 us
  waiting for transfers between devices: 46.7 us -> 0 us
  matrix products: 33.2 us -> 0 us
  blocking collectives: 20.4 us -> 0 us
  local copies, waits for them, and re-layouts: 27.5 us -> 7.58 us
  between operations: 14.4 us -> 0.66 us
  other arithmetic: 10.2 us -> 0 us
    all_to_all x8 -> x0, starting transfers between devices: 71.9 us -> none  [the longest x1 16.7 us: local(): lax.all_to_all(outgoing(value_rows), 'dp', split_axis=0, concat_axis=0, t...]
    pallas_call x0 -> x1, Pallas kernels: none -> 65.2 us  [local(): pl.pallas_call(functools.partial(kernel, peers, spans, rows, window), out...]
    all_to_all x8 -> x0, waiting for transfers between devices: 30 us -> none  [the longest x1 8.31 us: local(): lax.all_to_all(homeward(query_grads), 'dp', split_axis=0, concat_axis=0,...]
    dot_general x5 -> x0, matrix products: 28.9 us -> none  [the longest x1 10.5 us: local(): jnp.einsum('hqk,qhd->kd', dscore, query_three, preferred_element_type=jnp...]
    all_gather x2 -> x0, blocking collectives: 20.4 us -> none  [the longest x1 10.8 us: local(): lax.all_gather(value_here, 'seq', axis=0, tiled=True)]
    gather x8 -> x0, local copies, waits for them, and re-layouts: 17.1 us -> none  [the longest x4 8.9 us: settle(): return values.reshape(row_count, values.shape[2])[back_order][None]]
    unnamed x4 -> x0, waiting for transfers between devices: 16.7 us -> none
    unnamed x4 -> x16, local copies, waits for them, and re-layouts: 0.01 us -> 7.58 us
  transfers between devices with their start and end apart: 10 -> 0, of which waited for: 7 -> 0; matrix products, arithmetic and copies ran while one was open for 27% -> 0% of each run, Pallas kernels for 0% -> 0%
where the time goes in v1:
time: 73.7 us; the launch traced here: 73.4 us
  Pallas kernels  65.2 us (88%)
  local copies, waits for them, and re-layouts  7.58 us (10%)
    pallas_call x1, Pallas kernels, local(): pl.pallas_call(functools.partial(kernel, peers, spans, rows, window), out...  65.2 us
    unnamed x16, local copies, waits for them, and re-layouts  7.58 us

profile of v1, /device:TPU:1, one launch (start us, length us, event | category | flops | bytes accessed | tf_op | source)
XLA Modules:
  0.0 73.4 jit_solution(17513492179199042732)
XLA Ops:
  0.6 0.0 copy-start
  0.6 0.9 %copy-done = bf16[1,360,256]{2,1,0:T(8,128)(2,1)S(1)} copy-done((bf16[1,360,256]{2,1,0:T(8,128)(2,1)S(1)}, bf16[1,360,256]{2,1,0:T(8,128)(2,1)}, u32[]{:S(2)}) %copy-start) | copy-done | bytes 184344
  1.6 0.0 copy-start.1
  1.6 0.9 %copy-done.1 = bf16[1,360,256]{2,1,0:T(8,128)(2,1)S(1)} copy-done((bf16[1,360,256]{2,1,0:T(8,128)(2,1)S(1)}, bf16[1,360,256]{2,1,0:T(8,128)(2,1)}, u32[]{:S(2)}) %copy-start.1) | copy-done | bytes 184344
  2.5 0.0 copy-start.2
  2.5 0.9 %copy-done.2 = bf16[1,360,128]{2,1,0:T(8,128)(2,1)S(1)} copy-done((bf16[1,360,128]{2,1,0:T(8,128)(2,1)S(1)}, bf16[1,360,128]{2,1,0:T(8,128)(2,1)}, u32[]{:S(2)}) %copy-start.2) | copy-done | bytes 92184
  3.4 0.0 copy-start.3
  3.4 0.9 %copy-done.3 = bf16[1,360,128]{2,1,0:T(8,128)(2,1)S(1)} copy-done((bf16[1,360,128]{2,1,0:T(8,128)(2,1)S(1)}, bf16[1,360,128]{2,1,0:T(8,128)(2,1)}, u32[]{:S(2)}) %copy-start.3) | copy-done | bytes 92184
  4.3 0.0 copy-start.4
  4.3 0.7 copy-done.4
  4.9 0.0 copy-start.5
  4.9 0.7 copy-done.5
  5.6 65.2 %shard_map.93 = (bf16[1,360,256]{2,1,0:T(8,128)(2,1)S(1)}, bf16[1,360,256]{2,1,0:T(8,128)(2,1)S(1)}, bf16[1,360,128]{2,1,0:T(8,128)(2,1)S(1)}, bf16[1,360,128]{2,1,0:T(8,128)(2,1)S(1)}) custom-call(bf16[1,360,256]{2,1,0:T(8,128)(2,1)S(1)} %copy-done, bf16[1,360,128]{2,1,0:T(8,128)(2,1)S(1)} %copy-done.2, bf16[1,360,128]{2,1,0:T(8,128)(2,1)S(1)} %copy-done.3, ...), custom_call_target="tpu_custom_call" | custom-call | tf_op jit(solution)/shard_map/pallas_call | solution.py:300
  70.8 0.7 copy.14
  71.5 0.7 copy.15
  72.1 0.6 copy.16
  72.8 0.6 copy.17
Async XLA Ops:
  0.6 0.9 %copy-start = (bf16[1,360,256]{2,1,0:T(8,128)(2,1)S(1)}, bf16[1,360,256]{2,1,0:T(8,128)(2,1)}, u32[]{:S(2)}) copy-start(bf16[1,360,256]{2,1,0:T(8,128)(2,1)} %refs_0_.1) | copy-start | bytes 552964
  1.6 0.9 %copy-start.1 = (bf16[1,360,256]{2,1,0:T(8,128)(2,1)S(1)}, bf16[1,360,256]{2,1,0:T(8,128)(2,1)}, u32[]{:S(2)}) copy-start(bf16[1,360,256]{2,1,0:T(8,128)(2,1)} %refs_3_.1) | copy-start | bytes 552964
  2.5 0.9 %copy-start.2 = (bf16[1,360,128]{2,1,0:T(8,128)(2,1)S(1)}, bf16[1,360,128]{2,1,0:T(8,128)(2,1)}, u32[]{:S(2)}) copy-start(bf16[1,360,128]{2,1,0:T(8,128)(2,1)} %refs_1_.1) | copy-start | bytes 276484
  3.4 0.9 %copy-start.3 = (bf16[1,360,128]{2,1,0:T(8,128)(2,1)S(1)}, bf16[1,360,128]{2,1,0:T(8,128)(2,1)}, u32[]{:S(2)}) copy-start(bf16[1,360,128]{2,1,0:T(8,128)(2,1)} %refs_2_.1) | copy-start | bytes 276484
  4.3 0.7 copy-start.4
  4.9 0.7 copy-start.5

commit v2 on v1

--- a/solution.py
+++ b/solution.py
@@ -31,12 +31,15 @@
 
 def kernel(peers, spans, rows, window, *refs):
     (q_ref, k_ref, v_ref, dy_ref, len_ref, dest_ref, o_ref, dq_ref, dk_ref, dv_ref,
-     xin, perm, unperm, sends, ctx, ctxt, recvs, homes, backs, gsend, grecv, acc,
-     sbuf, dbuf, keyf, queryf, insem, ssem, rsem, xssem, xrsem) = refs
+     lens, dests, xin, perm, unperm, sends, ctx, ctxt, recvs, homes, backs, gsend, grecv, acc,
+     sbuf, dbuf, keyf, queryf, outs, insem, outsem, ssem, rsem, xssem, xrsem) = refs
     me = lax.axis_index("dp")
     shard = lax.axis_index("seq")
     group = rows // peers
     padded = peers * PAD
+
+    dest_load = pltpu.make_async_copy(dest_ref, dests, insem.at[6])
+    dest_load.start()
 
     tail = padded - PAD * ((padded - rows + PAD - 1) // PAD)
     xin[pl.ds(tail, padded - tail), :] = jnp.zeros((padded - tail, 6 * HEAD), BF16)
@@ -56,6 +59,8 @@
     ]
     for load in loads:
         load.start()
+    lens_load = pltpu.make_async_copy(len_ref, lens, insem.at[7])
+    lens_load.start()
 
     barrier = pltpu.get_barrier_semaphore()
 
@@ -71,7 +76,8 @@
             barrier, inc=1, device_id={"seq": lax.rem(shard + step, spans)}, device_id_type=MESH
         )
 
-    dest = dest_ref[...]
+    dest_load.wait()
+    dest = dests[...]
     is_dest = (lax.broadcasted_iota(jnp.int32, (peers, rows), 0) == dest).astype(F32)
     before = (
         lax.broadcasted_iota(jnp.int32, (rows, rows), 0)
@@ -124,9 +130,10 @@
         exchange(phase, sends.at[phase], landing[phase])
 
     unperm[...] = perm[...].T.astype(BF16)
-    bounds = [len_ref[0, 0]]
+    lens_load.wait()
+    bounds = [lens[0, 0]]
     for entry in range(1, DOCS):
-        bounds.append(bounds[-1] + len_ref[0, entry])
+        bounds.append(bounds[-1] + lens[0, entry])
 
     slot_row = lax.broadcasted_iota(jnp.int32, (padded, HEAD), 0)
     column = lax.broadcasted_iota(jnp.int32, (padded, HEAD), 1)
@@ -154,23 +161,38 @@
     arrived(0, landing[0])
 
     def forward(back):
+        near = back < spans - 1
         return pltpu.make_async_remote_copy(
-            src_ref=ctx.at[pl.ds(0, padded)],
+            src_ref=ctx.at[pl.ds((back - 1 if near else 0) * padded, padded)],
             dst_ref=ctx.at[pl.ds(back * padded, padded)],
             send_sem=xssem.at[back],
             recv_sem=xrsem.at[back],
-            device_id={"seq": lax.rem(shard + back, spans)},
+            device_id={"seq": lax.rem(shard + (1 if near else back), spans)},
             device_id_type=MESH,
         )
 
-    for back in range(1, spans):
-        @pl.when(shard + back < spans)
+    def forwards(back):
+        if back < spans - 1:
+            return (shard >= back - 1) & (shard + 1 < spans)
+        return shard + back < spans
+
+    def pass_on(back):
+        @pl.when(forwards(back))
         def _():
             forward(back).start()
-    for back in range(1, spans):
+
+    def take(back):
         @pl.when(shard >= back)
         def _():
             forward(back).wait_recv()
+
+    pass_on(1)
+    pass_on(spans - 1)
+    for back in range(1, spans - 1):
+        take(back)
+        if back + 1 < spans - 1:
+            pass_on(back + 1)
+    take(spans - 1)
     for back in range(spans):
         block = pl.ds(back * padded, padded)
         ctxt[:, block] = ctx[block, :].astype(F32).T.astype(BF16)
@@ -240,52 +262,83 @@
     attend(1)
 
     def give(back):
+        near = back < spans - 1
         return pltpu.make_async_remote_copy(
             src_ref=gsend.at[back],
             dst_ref=grecv.at[back],
             send_sem=xssem.at[spans + back],
             recv_sem=xrsem.at[spans + back],
-            device_id={"seq": lax.rem(shard + spans - back, spans)},
+            device_id={"seq": lax.rem(shard + spans - (1 if near else back), spans)},
             device_id_type=MESH,
         )
+
+    def gets(back):
+        if back < spans - 1:
+            return (shard + 1 < spans) & (shard + 1 >= back)
+        return shard + back < spans
 
     for back in range(spans - 1, -1, -1):
         gsend[back] = acc[pl.ds(back * padded, padded), :].astype(BF16)
+        if 0 < back < spans - 2:
+            @pl.when(gets(back + 1))
+            def _():
+                give(back + 1).wait_recv()
+                gsend[back] = (gsend[back].astype(F32) + grecv[back + 1].astype(F32)).astype(BF16)
         if back > 0:
             @pl.when(shard >= back)
             def _():
                 give(back).start()
     acc[pl.ds(0, padded), :] = gsend[0].astype(F32)
-    for back in range(1, spans):
-        @pl.when(shard + back < spans)
+    for back in (spans - 1, 1):
+        @pl.when(gets(back))
         def _():
             give(back).wait_recv()
             acc[pl.ds(0, padded), :] += grecv[back].astype(F32)
     homes[2] = acc[pl.ds(0, padded), :].astype(BF16)
     exchange(5, homes.at[2], backs.at[2])
 
-    def settle(member):
+    homeward = []
+
+    def settle(member, first, second, at):
         arrived(3 + member, backs.at[member])
-        return dot(unperm[...], backs[member]).astype(BF16)
-
-    for member in range(2):
-        rows_home = settle(member)
-        o_ref[0, :, pl.ds(member * HEAD, HEAD)] = rows_home[:rows, :HEAD]
-        dq_ref[0, :, pl.ds(member * HEAD, HEAD)] = rows_home[:rows, HEAD:]
-    rows_home = settle(2)
-    dk_ref[0] = rows_home[:rows, :HEAD]
-    dv_ref[0] = rows_home[:rows, HEAD:]
+        outs[member] = dot(unperm[...], backs[member]).astype(BF16)
+        for half, out in enumerate((first, second)):
+            store = pltpu.make_async_copy(
+                outs.at[member, pl.ds(0, rows), pl.ds(half * HEAD, HEAD)],
+                out.at[0, :, pl.ds(at, HEAD)],
+                outsem.at[2 * member + half],
+            )
+            store.start()
+            homeward.append(store)
+
+    settle(0, o_ref, dq_ref, 0)
+    settle(1, o_ref, dq_ref, HEAD)
+    settle(2, dk_ref, dv_ref, 0)
 
     for phase in range(3):
         departed(phase, sends.at[phase])
         departed(3 + phase, homes.at[phase])
     for back in range(1, spans):
-        @pl.when(shard + back < spans)
+        @pl.when(forwards(back))
         def _():
             forward(back).wait_send()
         @pl.when(shard >= back)
         def _():
             give(back).wait_send()
+    for store in homeward:
+        store.wait()
+
+
+def deliver(*refs):
+    sources, targets, sem = refs[:4], refs[4:8], refs[8]
+    copies = [
+        pltpu.make_async_copy(source, target, sem.at[at])
+        for at, (source, target) in enumerate(zip(sources, targets))
+    ]
+    for copy in copies:
+        copy.start()
+    for copy in copies:
+        copy.wait()
 
 
 def solution(mesh, window=WINDOW):
@@ -295,19 +348,18 @@
         rows = queries.shape[1]
         padded = peers * PAD
         blocks = spans * padded
-        whole = pl.BlockSpec(memory_space=pltpu.VMEM)
         loose = pl.BlockSpec(memory_space=pl.ANY)
-        return pl.pallas_call(
+        shapes = tuple(
+            jax.ShapeDtypeStruct((1, rows, columns), BF16) for columns in (PAIR, PAIR, HEAD, HEAD)
+        )
+        landed = pl.pallas_call(
             functools.partial(kernel, peers, spans, rows, window),
-            out_shape=(
-                jax.ShapeDtypeStruct((1, rows, PAIR), BF16),
-                jax.ShapeDtypeStruct((1, rows, PAIR), BF16),
-                jax.ShapeDtypeStruct((1, rows, HEAD), BF16),
-                jax.ShapeDtypeStruct((1, rows, HEAD), BF16),
-            ),
-            in_specs=[loose] * 4 + [pl.BlockSpec(memory_space=pltpu.SMEM), whole],
-            out_specs=(whole,) * 4,
+            out_shape=shapes,
+            in_specs=[loose] * 6,
+            out_specs=(loose,) * 4,
             scratch_shapes=[
+                pltpu.SMEM((1, DOCS), jnp.int32),
+                pltpu.VMEM((1, rows), jnp.int32),
                 pltpu.VMEM((padded, 6 * HEAD), BF16),
                 pltpu.VMEM((padded, padded), F32),
                 pltpu.VMEM((padded, padded), BF16),
@@ -324,6 +376,8 @@
                 pltpu.VMEM((blocks, padded), F32),
                 pltpu.VMEM((blocks, HEAD), BF16),
                 pltpu.VMEM((padded, HEAD), BF16),
+                pltpu.VMEM((3, padded, PAIR), BF16),
+                pltpu.SemaphoreType.DMA((8,)),
                 pltpu.SemaphoreType.DMA((6,)),
                 pltpu.SemaphoreType.DMA((6,)),
                 pltpu.SemaphoreType.DMA((6,)),
@@ -331,9 +385,16 @@
                 pltpu.SemaphoreType.DMA((2 * spans,)),
             ],
             compiler_params=pltpu.CompilerParams(
-                collective_id=0, has_side_effects=True, vmem_limit_bytes=40 << 20
+                collective_id=0, has_side_effects=True, vmem_limit_bytes=60 << 20
             ),
         )(queries, key_rows, value_rows, grad_out, doc_lengths, dest_index)
+        return pl.pallas_call(
+            deliver,
+            out_shape=shapes,
+            in_specs=[loose] * 4,
+            out_specs=(loose,) * 4,
+            scratch_shapes=[pltpu.SemaphoreType.DMA((4,))],
+        )(*landed)
 
     wide = P("dp", "seq", "head")
     return jax.shard_map(

time: 73.7 us -> 83 us (1.13)
  Pallas kernels: 65.2 us -> 81.7 us
  local copies, waits for them, and re-layouts: 7.58 us -> 0 us
    pallas_call x0 -> x1, Pallas kernels: none -> 17.9 us  [local(): pl.pallas_call(deliver, out_shape=shapes, in_specs=[loose] * 4, out_specs...]
    unnamed x16 -> x0, local copies, waits for them, and re-layouts: 7.58 us -> none
    pallas_call x1, Pallas kernels: 65.2 us -> 63.8 us  [local(): pl.pallas_call(functools.partial(kernel, peers, spans, rows, window), out...]
where the time goes in v2:
time: 83 us; the launch traced here: 82.4 us
  Pallas kernels  81.7 us (98%)
    pallas_call x1, Pallas kernels, local(): pl.pallas_call(functools.partial(kernel, peers, spans, rows, window), out...  63.8 us
    pallas_call x1, Pallas kernels, local(): pl.pallas_call(deliver, out_shape=shapes, in_specs=[loose] * 4, out_specs...  17.9 us

profile of v2, /device:TPU:1, one launch (start us, length us, event | category | flops | bytes accessed | tf_op | source)
XLA Modules:
  0.0 82.4 jit_solution(13799636691157112663)
XLA Ops:
  0.6 63.8 %shard_map.93 = (bf16[1,360,256]{2,1,0:T(8,128)(2,1)}, bf16[1,360,256]{2,1,0:T(8,128)(2,1)}, bf16[1,360,128]{2,1,0:T(8,128)(2,1)}, bf16[1,360,128]{2,1,0:T(8,128)(2,1)}) custom-call(bf16[1,360,256]{2,1,0:T(8,128)(2,1)} %refs_0_.1, bf16[1,360,128]{2,1,0:T(8,128)(2,1)} %refs_1_.1, bf16[1,360,128]{2,1,0:T(8,128)(2,1)} %refs_2_.1, bf16[1,360,256]{2,1,0:T(8,128)(2,1)} %refs_3_.1, ...), custom_call_target="tpu_custom_call" | custom-call | tf_op jit(solution)/shard_map/pallas_call | solution.py:355
  64.5 17.9 %shard_map.94 = (bf16[1,360,256]{2,1,0:T(8,128)(2,1)}, bf16[1,360,256]{2,1,0:T(8,128)(2,1)}, bf16[1,360,128]{2,1,0:T(8,128)(2,1)}, bf16[1,360,128]{2,1,0:T(8,128)(2,1)}) custom-call(bf16[1,360,256]{2,1,0:T(8,128)(2,1)} %get-tuple-element.8.refs_0_, bf16[1,360,256]{2,1,0:T(8,128)(2,1)} %get-tuple-element.9.refs_1_, ...), custom_call_target="tpu_custom_call" | custom-call | tf_op jit(solution)/shard_map/pallas_call | solution.py:391

commit v3 on v2

--- a/solution.py
+++ b/solution.py
@@ -330,15 +330,23 @@
 
 
 def deliver(*refs):
-    sources, targets, sem = refs[:4], refs[4:8], refs[8]
-    copies = [
-        pltpu.make_async_copy(source, target, sem.at[at])
-        for at, (source, target) in enumerate(zip(sources, targets))
+    sources, targets, holds = refs[:4], refs[4:8], refs[8:12]
+    insem, outsem = refs[12:]
+    loads = [
+        pltpu.make_async_copy(source, hold, insem.at[at])
+        for at, (source, hold) in enumerate(zip(sources, holds))
     ]
-    for copy in copies:
-        copy.start()
-    for copy in copies:
-        copy.wait()
+    stores = [
+        pltpu.make_async_copy(hold, target, outsem.at[at])
+        for at, (hold, target) in enumerate(zip(holds, targets))
+    ]
+    for load in loads:
+        load.start()
+    for load, store in zip(loads, stores):
+        load.wait()
+        store.start()
+    for store in stores:
+        store.wait()
 
 
 def solution(mesh, window=WINDOW):
@@ -393,7 +401,11 @@
             out_shape=shapes,
             in_specs=[loose] * 4,
             out_specs=(loose,) * 4,
-            scratch_shapes=[pltpu.SemaphoreType.DMA((4,))],
+            scratch_shapes=[
+                *(pltpu.VMEM(shape.shape, BF16) for shape in shapes),
+                pltpu.SemaphoreType.DMA((4,)),
+                pltpu.SemaphoreType.DMA((4,)),
+            ],
         )(*landed)
 
     wide = P("dp", "seq", "head")

time: 83 us -> 67 us (0.81)
  Pallas kernels: 81.7 us -> 65.7 us
    pallas_call x1, Pallas kernels: 17.9 us -> 1.82 us  [local(): pl.pallas_call(deliver, out_shape=shapes, in_specs=[loose] * 4, out_specs...]
where the time goes in v3:
time: 67 us; the launch traced here: 66.3 us
  Pallas kernels  65.7 us (98%)
    pallas_call x1, Pallas kernels, local(): pl.pallas_call(functools.partial(kernel, peers, spans, rows, window), out...  63.8 us
    pallas_call x1, Pallas kernels, local(): pl.pallas_call(deliver, out_shape=shapes, in_specs=[loose] * 4, out_specs...  1.82 us

profile of v3, /device:TPU:1, one launch (start us, length us, event | category | flops | bytes accessed | tf_op | source)
XLA Modules:
  0.0 66.3 jit_solution(6680147566975116857)
XLA Ops:
  0.6 63.8 %shard_map.93 = (bf16[1,360,256]{2,1,0:T(8,128)(2,1)}, bf16[1,360,256]{2,1,0:T(8,128)(2,1)}, bf16[1,360,128]{2,1,0:T(8,128)(2,1)}, bf16[1,360,128]{2,1,0:T(8,128)(2,1)}) custom-call(bf16[1,360,256]{2,1,0:T(8,128)(2,1)} %refs_0_.1, bf16[1,360,128]{2,1,0:T(8,128)(2,1)} %refs_1_.1, bf16[1,360,128]{2,1,0:T(8,128)(2,1)} %refs_2_.1, bf16[1,360,256]{2,1,0:T(8,128)(2,1)} %refs_3_.1, ...), custom_call_target="tpu_custom_call" | custom-call | tf_op jit(solution)/shard_map/pallas_call | solution.py:363
  64.5 1.8 %shard_map.94 = (bf16[1,360,256]{2,1,0:T(8,128)(2,1)}, bf16[1,360,256]{2,1,0:T(8,128)(2,1)}, bf16[1,360,128]{2,1,0:T(8,128)(2,1)}, bf16[1,360,128]{2,1,0:T(8,128)(2,1)}) custom-call(bf16[1,360,256]{2,1,0:T(8,128)(2,1)} %get-tuple-element.8.refs_0_, bf16[1,360,256]{2,1,0:T(8,128)(2,1)} %get-tuple-element.9.refs_1_, ...), custom_call_target="tpu_custom_call" | custom-call | tf_op jit(solution)/shard_map/pallas_call | solution.py:399

commit v4 on v3

--- a/solution.py
+++ b/solution.py
@@ -32,11 +32,12 @@
 def kernel(peers, spans, rows, window, *refs):
     (q_ref, k_ref, v_ref, dy_ref, len_ref, dest_ref, o_ref, dq_ref, dk_ref, dv_ref,
      lens, dests, xin, perm, unperm, sends, ctx, ctxt, recvs, homes, backs, gsend, grecv, acc,
-     sbuf, dbuf, keyf, queryf, outs, insem, outsem, ssem, rsem, xssem, xrsem) = refs
+     sbuf, dbuf, gaps, keyf, queryf, outs, insem, outsem, ssem, rsem, xssem, xrsem) = refs
     me = lax.axis_index("dp")
     shard = lax.axis_index("seq")
     group = rows // peers
     padded = peers * PAD
+    pieces = peers // 2
 
     dest_load = pltpu.make_async_copy(dest_ref, dests, insem.at[6])
     dest_load.start()
@@ -93,7 +94,7 @@
     perm[:, pl.ds(0, rows)] = hot
     perm_low = perm[...].astype(BF16)
 
-    def exchange(phase, src, dst):
+    def exchange(phase, src, dst, first=0, last=peers - 1, beside=None):
         def one(step, carry):
             odd = lax.rem(step, 2)
             far = peers // 2 - (step + 1) // 2
@@ -107,9 +108,13 @@
                 device_id={"dp": peer},
                 device_id_type=MESH,
             ).start()
+            if beside is not None:
+                beside(step - first)
             return carry
 
-        lax.fori_loop(0, peers - 1, one, 0)
+        lax.fori_loop(first, last, one, 0)
+        if first > 0:
+            return
         own = pl.ds(pl.multiple_of(me * PAD, PAD), PAD)
         pltpu.make_async_copy(src.at[own], dst.at[own], rsem.at[phase]).start()
 
@@ -145,6 +150,12 @@
         for bound in bounds:
             total = total + (position >= bound).astype(jnp.int32)
         return total
+
+    def spot(axis):
+        index = lax.broadcasted_iota(jnp.int32, (padded, padded), axis)
+        return (index // PAD) * group + lax.rem(index, PAD)
+
+    gaps[...] = (spot(1) - spot(0)).astype(F32)
 
     queryf[...] = (documents(local + shard * rows) == column).astype(F32).astype(BF16)
     for back in range(spans):
@@ -161,47 +172,29 @@
     arrived(0, landing[0])
 
     def forward(back):
-        near = back < spans - 1
         return pltpu.make_async_remote_copy(
-            src_ref=ctx.at[pl.ds((back - 1 if near else 0) * padded, padded)],
+            src_ref=ctx.at[pl.ds(0, padded)],
             dst_ref=ctx.at[pl.ds(back * padded, padded)],
             send_sem=xssem.at[back],
             recv_sem=xrsem.at[back],
-            device_id={"seq": lax.rem(shard + (1 if near else back), spans)},
+            device_id={"seq": lax.rem(shard + back, spans)},
             device_id_type=MESH,
         )
 
     def forwards(back):
-        if back < spans - 1:
-            return (shard >= back - 1) & (shard + 1 < spans)
         return shard + back < spans
 
-    def pass_on(back):
+    for back in range(1, spans):
         @pl.when(forwards(back))
         def _():
             forward(back).start()
-
-    def take(back):
+    for back in range(1, spans):
         @pl.when(shard >= back)
         def _():
             forward(back).wait_recv()
-
-    pass_on(1)
-    pass_on(spans - 1)
-    for back in range(1, spans - 1):
-        take(back)
-        if back + 1 < spans - 1:
-            pass_on(back + 1)
-    take(spans - 1)
     for back in range(spans):
         block = pl.ds(back * padded, padded)
         ctxt[:, block] = ctx[block, :].astype(F32).T.astype(BF16)
-
-    key_row = lax.broadcasted_iota(jnp.int32, (padded, padded), 0)
-    query_col = lax.broadcasted_iota(jnp.int32, (padded, padded), 1)
-
-    def spot(index):
-        return (index // PAD) * group + lax.rem(index, PAD)
 
     def attend(member):
         arrived(1 + member, landing[1 + member])
@@ -214,80 +207,86 @@
             key_wide = jnp.concatenate([ctx[block, pl.ds(0, HEAD)], keyf[block, :]], axis=1)
             scores = dot_nt(key_wide, query_wide)
             if back == 0:
-                scores = jnp.where(query_col >= key_row, scores, NEG)
+                scores = jnp.where(gaps[...] >= 0, scores, NEG)
             if back * rows + rows - 1 >= window:
-                gap = back * rows + spot(query_col) - spot(key_row)
-                scores = jnp.where(gap < window, scores, NEG)
+                scores = jnp.where(gaps[...] < window - back * rows, scores, NEG)
             sbuf[block, :] = scores
             top = jnp.max(scores, axis=0, keepdims=True)
             peak = top if peak is None else jnp.maximum(peak, top)
         total = jnp.zeros((1, padded), F32)
+        mixed = jnp.zeros((HEAD, padded), F32)
+        center = jnp.zeros((1, padded), F32)
         for back in range(spans):
             block = pl.ds(back * padded, padded)
             weight = jnp.exp2((sbuf[block, :] - peak) * (SCALE * LOG2E))
             sbuf[block, :] = weight
             total = total + jnp.sum(weight, axis=0, keepdims=True)
+            dprob = dot_nt(ctx[block, pl.ds(HEAD, HEAD)], grad)
+            dbuf[block, :] = dprob
+            center = center + jnp.sum(weight * dprob, axis=0, keepdims=True)
+            mixed = mixed + dot(ctxt[pl.ds(HEAD, HEAD), block], weight.astype(BF16))
         share = 1.0 / total
-        mixed = jnp.zeros((HEAD, padded), F32)
-        center = jnp.zeros((1, padded), F32)
+        mixed = mixed * share
+        center = center * share
+        dquery = jnp.zeros((HEAD, padded), F32)
         for back in range(spans):
             block = pl.ds(back * padded, padded)
             prob = sbuf[block, :] * share
-            sbuf[block, :] = prob
-            low = prob.astype(BF16)
-            dprob = dot_nt(ctx[block, pl.ds(HEAD, HEAD)], grad)
-            dbuf[block, :] = dprob
-            center = center + jnp.sum(prob * dprob, axis=0, keepdims=True)
-            mixed = mixed + dot(ctxt[pl.ds(HEAD, HEAD), block], low)
-            part = dot(low, grad)
-            if member == 0:
-                acc[block, pl.ds(HEAD, HEAD)] = part
-            else:
-                acc[block, pl.ds(HEAD, HEAD)] += part
-        dquery = jnp.zeros((HEAD, padded), F32)
-        for back in range(spans):
-            block = pl.ds(back * padded, padded)
-            dscore = (sbuf[block, :] * (dbuf[block, :] - center)).astype(BF16)
+            dscore = (prob * (dbuf[block, :] - center)).astype(BF16)
             dquery = dquery + dot(ctxt[pl.ds(0, HEAD), block], dscore)
-            part = dot(dscore, query) * SCALE
-            if member == 0:
-                acc[block, pl.ds(0, HEAD)] = part
-            else:
-                acc[block, pl.ds(0, HEAD)] += part
+            for at, part in (
+                (0, dot(dscore, query) * SCALE),
+                (HEAD, dot(prob.astype(BF16), grad)),
+            ):
+                if member == 0:
+                    acc[block, pl.ds(at, HEAD)] = part
+                else:
+                    part = acc[block, pl.ds(at, HEAD)] + part
+                    gsend[back, :, pl.ds(at, HEAD)] = part.astype(BF16)
         homes[member, :, pl.ds(0, HEAD)] = mixed.T.astype(BF16)
         homes[member, :, pl.ds(HEAD, HEAD)] = (dquery * SCALE).T.astype(BF16)
-        exchange(3 + member, homes.at[member], backs.at[member])
 
     attend(0)
+    exchange(3, homes.at[0], backs.at[0])
     attend(1)
 
-    def give(back):
+    def give(back, start=0, size=padded):
         near = back < spans - 1
+        start = pl.multiple_of(start, PAD)
         return pltpu.make_async_remote_copy(
-            src_ref=gsend.at[back],
-            dst_ref=grecv.at[back],
+            src_ref=gsend.at[back, pl.ds(start, size)],
+            dst_ref=grecv.at[back, pl.ds(start, size)],
             send_sem=xssem.at[spans + back],
             recv_sem=xrsem.at[spans + back],
             device_id={"seq": lax.rem(shard + spans - (1 if near else back), spans)},
             device_id_type=MESH,
         )
 
+    def give_on(*backs):
+        def piece(index):
+            for back in backs:
+                @pl.when(shard >= back)
+                def _():
+                    give(back, index * (padded // pieces), padded // pieces).start()
+
+        return piece
+
     def gets(back):
         if back < spans - 1:
             return (shard + 1 < spans) & (shard + 1 >= back)
         return shard + back < spans
 
-    for back in range(spans - 1, -1, -1):
-        gsend[back] = acc[pl.ds(back * padded, padded), :].astype(BF16)
-        if 0 < back < spans - 2:
-            @pl.when(gets(back + 1))
-            def _():
-                give(back + 1).wait_recv()
-                gsend[back] = (gsend[back].astype(F32) + grecv[back + 1].astype(F32)).astype(BF16)
-        if back > 0:
-            @pl.when(shard >= back)
-            def _():
-                give(back).start()
+    exchange(4, homes.at[1], backs.at[1], 0, pieces, give_on(spans - 1, 2))
+
+    @pl.when(gets(2))
+    def _():
+        give(2).wait_recv()
+        gsend[1] = (gsend[1].astype(F32) + grecv[2].astype(F32)).astype(BF16)
+
+    rest = peers - 1 - pieces
+    exchange(4, homes.at[1], backs.at[1], pieces, peers - 1, give_on(1))
+    for index in range(rest, pieces):
+        give_on(1)(index)
     acc[pl.ds(0, padded), :] = gsend[0].astype(F32)
     for back in (spans - 1, 1):
         @pl.when(gets(back))
@@ -382,6 +381,7 @@
                 pltpu.VMEM((blocks, PAIR), F32),
                 pltpu.VMEM((blocks, padded), F32),
                 pltpu.VMEM((blocks, padded), F32),
+                pltpu.VMEM((padded, padded), F32),
                 pltpu.VMEM((blocks, HEAD), BF16),
                 pltpu.VMEM((padded, HEAD), BF16),
                 pltpu.VMEM((3, padded, PAIR), BF16),

time: 67 us -> 66 us (0.985)
  no operation moved by 1% of the time
where the time goes in v4:
time: 66 us; the launch traced here: 65.8 us
  Pallas kernels  65.2 us (99%)
    pallas_call x1, Pallas kernels, local(): pl.pallas_call(functools.partial(kernel, peers, spans, rows, window), out...  63.3 us
    pallas_call x1, Pallas kernels, local(): pl.pallas_call(deliver, out_shape=shapes, in_specs=[loose] * 4, out_specs...  1.82 us

profile of v4, /device:TPU:1, one launch (start us, length us, event | category | flops | bytes accessed | tf_op | source)
XLA Modules:
  0.0 65.8 jit_solution(14466433629410233714)
XLA Ops:
  0.6 63.3 %shard_map.93 = (bf16[1,360,256]{2,1,0:T(8,128)(2,1)}, bf16[1,360,256]{2,1,0:T(8,128)(2,1)}, bf16[1,360,128]{2,1,0:T(8,128)(2,1)}, bf16[1,360,128]{2,1,0:T(8,128)(2,1)}) custom-call(bf16[1,360,256]{2,1,0:T(8,128)(2,1)} %refs_0_.1, bf16[1,360,128]{2,1,0:T(8,128)(2,1)} %refs_1_.1, bf16[1,360,128]{2,1,0:T(8,128)(2,1)} %refs_2_.1, bf16[1,360,256]{2,1,0:T(8,128)(2,1)} %refs_3_.1, ...), custom_call_target="tpu_custom_call" | custom-call | tf_op jit(solution)/shard_map/pallas_call | solution.py:362
  64.0 1.8 %shard_map.94 = (bf16[1,360,256]{2,1,0:T(8,128)(2,1)}, bf16[1,360,256]{2,1,0:T(8,128)(2,1)}, bf16[1,360,128]{2,1,0:T(8,128)(2,1)}, bf16[1,360,128]{2,1,0:T(8,128)(2,1)}) custom-call(bf16[1,360,256]{2,1,0:T(8,128)(2,1)} %get-tuple-element.8.refs_0_, bf16[1,360,256]{2,1,0:T(8,128)(2,1)} %get-tuple-element.9.refs_1_, ...), custom_call_target="tpu_custom_call" | custom-call | tf_op jit(solution)/shard_map/pallas_call | solution.py:399

commit v5 on v4

--- a/solution.py
+++ b/solution.py
@@ -13,6 +13,7 @@
 PAD = 16
 WINDOW = 1024
 DOCS = 4
+MIDDLE = 8
 SCALE = 168.0 ** (-0.5)
 LOG2E = 1.0 / math.log(2.0)
 NEG = -1e30
@@ -37,7 +38,6 @@
     shard = lax.axis_index("seq")
     group = rows // peers
     padded = peers * PAD
-    pieces = peers // 2
 
     dest_load = pltpu.make_async_copy(dest_ref, dests, insem.at[6])
     dest_load.start()
@@ -94,7 +94,7 @@
     perm[:, pl.ds(0, rows)] = hot
     perm_low = perm[...].astype(BF16)
 
-    def exchange(phase, src, dst, first=0, last=peers - 1, beside=None):
+    def exchange(phase, src, dst, first=0, last=peers - 1):
         def one(step, carry):
             odd = lax.rem(step, 2)
             far = peers // 2 - (step + 1) // 2
@@ -108,8 +108,6 @@
                 device_id={"dp": peer},
                 device_id_type=MESH,
             ).start()
-            if beside is not None:
-                beside(step - first)
             return carry
 
         lax.fori_loop(first, last, one, 0)
@@ -125,14 +123,29 @@
         sent = src.at[pl.ds(0, padded - PAD)]
         pltpu.make_async_copy(sent, sent, ssem.at[phase]).wait()
 
-    landing = (ctx.at[pl.ds(0, padded)], recvs.at[0], recvs.at[1])
-    for phase in range(3):
-        loads[2 * phase].wait()
-        loads[2 * phase + 1].wait()
-        sends[phase] = dot(perm_low, xin[:, pl.ds(phase * PAIR, PAIR)]).astype(BF16)
+    half = (pl.ds(0, HEAD), pl.ds(HEAD, HEAD))
+    landing = {
+        0: ctx.at[pl.ds(0, padded), half[0]],
+        6: ctx.at[pl.ds(0, padded), half[1]],
+        1: recvs.at[0],
+        2: recvs.at[1],
+    }
+    leaving = {0: sends.at[0, :, half[0]], 6: sends.at[0, :, half[1]], 1: sends.at[1], 2: sends.at[2]}
+    returning = {
+        3: (homes.at[0, :, half[0]], backs.at[0, :, half[0]]),
+        7: (homes.at[0, :, half[1]], backs.at[0, :, half[1]]),
+        4: (homes.at[1], backs.at[1]),
+        5: (homes.at[2, :, half[0]], backs.at[2, :, half[0]]),
+        8: (homes.at[2, :, half[1]], backs.at[2, :, half[1]]),
+    }
+    for phase, first, count in ((0, 0, 1), (6, 1, 1), (1, 2, 2), (2, 4, 2)):
+        for entry in range(first, first + count):
+            loads[entry].wait()
+        columns = pl.ds(first * HEAD, count * HEAD)
+        leaving[phase][...] = dot(perm_low, xin[:, columns]).astype(BF16)
         if phase == 0:
             pl.semaphore_wait(barrier, peers - 1 + spans - 1)
-        exchange(phase, sends.at[phase], landing[phase])
+        exchange(phase, leaving[phase], landing[phase])
 
     unperm[...] = perm[...].T.astype(BF16)
     lens_load.wait()
@@ -169,14 +182,12 @@
         def _():
             ctx[pl.ds(back * padded, padded)] = jnp.zeros((padded, PAIR), BF16)
 
-    arrived(0, landing[0])
-
-    def forward(back):
+    def forward(back, side):
         return pltpu.make_async_remote_copy(
-            src_ref=ctx.at[pl.ds(0, padded)],
-            dst_ref=ctx.at[pl.ds(back * padded, padded)],
-            send_sem=xssem.at[back],
-            recv_sem=xrsem.at[back],
+            src_ref=ctx.at[pl.ds(0, padded), half[side]],
+            dst_ref=ctx.at[pl.ds(back * padded, padded), half[side]],
+            send_sem=xssem.at[(2 * side) * spans + back],
+            recv_sem=xrsem.at[(2 * side) * spans + back],
             device_id={"seq": lax.rem(shard + back, spans)},
             device_id_type=MESH,
         )
@@ -184,19 +195,25 @@
     def forwards(back):
         return shard + back < spans
 
-    for back in range(1, spans):
-        @pl.when(forwards(back))
-        def _():
-            forward(back).start()
-    for back in range(1, spans):
-        @pl.when(shard >= back)
-        def _():
-            forward(back).wait_recv()
-    for back in range(spans):
-        block = pl.ds(back * padded, padded)
-        ctxt[:, block] = ctx[block, :].astype(F32).T.astype(BF16)
+    for side, phase in enumerate((0, 6)):
+        arrived(phase, landing[phase])
+        for back in range(1, spans):
+            @pl.when(forwards(back))
+            def _():
+                forward(back, side).start()
+
+    def gathered(side):
+        for back in range(1, spans):
+            @pl.when(shard >= back)
+            def _():
+                forward(back, side).wait_recv()
+        for back in range(spans):
+            block = pl.ds(back * padded, padded)
+            ctxt[half[side], block] = ctx[block, half[side]].astype(F32).T.astype(BF16)
 
     def attend(member):
+        if member == 0:
+            gathered(0)
         arrived(1 + member, landing[1 + member])
         query = recvs[member, :, pl.ds(0, HEAD)]
         grad = recvs[member, :, pl.ds(HEAD, HEAD)]
@@ -213,6 +230,8 @@
             sbuf[block, :] = scores
             top = jnp.max(scores, axis=0, keepdims=True)
             peak = top if peak is None else jnp.maximum(peak, top)
+        if member == 0:
+            gathered(1)
         total = jnp.zeros((1, padded), F32)
         mixed = jnp.zeros((HEAD, padded), F32)
         center = jnp.zeros((1, padded), F32)
@@ -226,7 +245,9 @@
             center = center + jnp.sum(weight * dprob, axis=0, keepdims=True)
             mixed = mixed + dot(ctxt[pl.ds(HEAD, HEAD), block], weight.astype(BF16))
         share = 1.0 / total
-        mixed = mixed * share
+        homes[member, :, pl.ds(0, HEAD)] = (mixed * share).T.astype(BF16)
+        if member == 0:
+            exchange(3, *returning[3])
         center = center * share
         dquery = jnp.zeros((HEAD, padded), F32)
         for back in range(spans):
@@ -243,87 +264,95 @@
                 else:
                     part = acc[block, pl.ds(at, HEAD)] + part
                     gsend[back, :, pl.ds(at, HEAD)] = part.astype(BF16)
-        homes[member, :, pl.ds(0, HEAD)] = mixed.T.astype(BF16)
         homes[member, :, pl.ds(HEAD, HEAD)] = (dquery * SCALE).T.astype(BF16)
+        if member == 0:
+            exchange(7, *returning[7])
 
     attend(0)
-    exchange(3, homes.at[0], backs.at[0])
     attend(1)
 
-    def give(back, start=0, size=padded):
+    def give(back, side):
         near = back < spans - 1
-        start = pl.multiple_of(start, PAD)
+        sem = (2 * side + 1) * spans + back
         return pltpu.make_async_remote_copy(
-            src_ref=gsend.at[back, pl.ds(start, size)],
-            dst_ref=grecv.at[back, pl.ds(start, size)],
-            send_sem=xssem.at[spans + back],
-            recv_sem=xrsem.at[spans + back],
+            src_ref=gsend.at[back, :, half[side]],
+            dst_ref=grecv.at[back, :, half[side]],
+            send_sem=xssem.at[sem],
+            recv_sem=xrsem.at[sem],
             device_id={"seq": lax.rem(shard + spans - (1 if near else back), spans)},
             device_id_type=MESH,
         )
 
-    def give_on(*backs):
-        def piece(index):
-            for back in backs:
-                @pl.when(shard >= back)
-                def _():
-                    give(back, index * (padded // pieces), padded // pieces).start()
-
-        return piece
+    def give_on(back, side):
+        @pl.when(shard >= back)
+        def _():
+            give(back, side).start()
 
     def gets(back):
         if back < spans - 1:
             return (shard + 1 < spans) & (shard + 1 >= back)
         return shard + back < spans
 
-    exchange(4, homes.at[1], backs.at[1], 0, pieces, give_on(spans - 1, 2))
-
-    @pl.when(gets(2))
-    def _():
-        give(2).wait_recv()
-        gsend[1] = (gsend[1].astype(F32) + grecv[2].astype(F32)).astype(BF16)
-
-    rest = peers - 1 - pieces
-    exchange(4, homes.at[1], backs.at[1], pieces, peers - 1, give_on(1))
-    for index in range(rest, pieces):
-        give_on(1)(index)
-    acc[pl.ds(0, padded), :] = gsend[0].astype(F32)
-    for back in (spans - 1, 1):
-        @pl.when(gets(back))
+    for side in (1, 0):
+        give_on(2, side)
+        give_on(spans - 1, side)
+    marks = (0, MIDDLE, 2 * MIDDLE, peers - 1)
+    exchange(4, *returning[4], marks[0], marks[1])
+    for side in (1, 0):
+        @pl.when(gets(2))
         def _():
-            give(back).wait_recv()
-            acc[pl.ds(0, padded), :] += grecv[back].astype(F32)
-    homes[2] = acc[pl.ds(0, padded), :].astype(BF16)
-    exchange(5, homes.at[2], backs.at[2])
+            give(2, side).wait_recv()
+            gsend[1, :, half[side]] = (
+                gsend[1, :, half[side]].astype(F32) + grecv[2, :, half[side]].astype(F32)
+            ).astype(BF16)
+
+        give_on(1, side)
+        exchange(4, *returning[4], marks[2 - side], marks[3 - side])
+    for side in (1, 0):
+        own = (pl.ds(0, padded), half[side])
+        acc[own] = gsend[0, :, half[side]].astype(F32)
+        for back in (spans - 1, 1):
+            @pl.when(gets(back))
+            def _():
+                give(back, side).wait_recv()
+                acc[own] += grecv[back, :, half[side]].astype(F32)
+        homes[2, :, half[side]] = acc[own].astype(BF16)
+        exchange(8 if side else 5, *returning[8 if side else 5])
 
     homeward = []
 
-    def settle(member, first, second, at):
-        arrived(3 + member, backs.at[member])
-        outs[member] = dot(unperm[...], backs[member]).astype(BF16)
-        for half, out in enumerate((first, second)):
+    def settle(member, phases, columns, stores):
+        for phase in phases:
+            arrived(phase, returning[phase][1])
+        outs[member, :, columns] = dot(unperm[...], backs[member, :, columns]).astype(BF16)
+        for side, out, at in stores:
             store = pltpu.make_async_copy(
-                outs.at[member, pl.ds(0, rows), pl.ds(half * HEAD, HEAD)],
+                outs.at[member, pl.ds(0, rows), half[side]],
                 out.at[0, :, pl.ds(at, HEAD)],
-                outsem.at[2 * member + half],
+                outsem.at[2 * member + side],
             )
             store.start()
             homeward.append(store)
 
-    settle(0, o_ref, dq_ref, 0)
-    settle(1, o_ref, dq_ref, HEAD)
-    settle(2, dk_ref, dv_ref, 0)
-
-    for phase in range(3):
-        departed(phase, sends.at[phase])
-        departed(3 + phase, homes.at[phase])
+    both = pl.ds(0, PAIR)
+    settle(0, (3, 7), both, ((0, o_ref, 0), (1, dq_ref, 0)))
+    settle(1, (4,), both, ((0, o_ref, HEAD), (1, dq_ref, HEAD)))
+    settle(2, (8,), half[1], ((1, dv_ref, 0),))
+    settle(2, (5,), half[0], ((0, dk_ref, 0),))
+
+    for phase, source in leaving.items():
+        departed(phase, source)
+    for phase, (source, _) in returning.items():
+        departed(phase, source)
     for back in range(1, spans):
         @pl.when(forwards(back))
         def _():
-            forward(back).wait_send()
+            forward(back, 0).wait_send()
+            forward(back, 1).wait_send()
         @pl.when(shard >= back)
         def _():
-            give(back).wait_send()
+            give(back, 0).wait_send()
+            give(back, 1).wait_send()
     for store in homeward:
         store.wait()
 
@@ -387,10 +416,10 @@
                 pltpu.VMEM((3, padded, PAIR), BF16),
                 pltpu.SemaphoreType.DMA((8,)),
                 pltpu.SemaphoreType.DMA((6,)),
-                pltpu.SemaphoreType.DMA((6,)),
-                pltpu.SemaphoreType.DMA((6,)),
-                pltpu.SemaphoreType.DMA((2 * spans,)),
-                pltpu.SemaphoreType.DMA((2 * spans,)),
+                pltpu.SemaphoreType.DMA((9,)),
+                pltpu.SemaphoreType.DMA((9,)),
+                pltpu.SemaphoreType.DMA((4 * spans,)),
+                pltpu.SemaphoreType.DMA((4 * spans,)),
             ],
             compiler_params=pltpu.CompilerParams(
                 collective_id=0, has_side_effects=True, vmem_limit_bytes=60 << 20

time: 66 us -> 64.3 us (0.974)
  Pallas kernels: 65.2 us -> 63.4 us
    pallas_call x1, Pallas kernels: 63.3 us -> 61.6 us  [local(): pl.pallas_call(functools.partial(kernel, peers, spans, rows, window), out...]
where the time goes in v5:
time: 64.3 us; the launch traced here: 64.1 us
  Pallas kernels  63.4 us (99%)
    pallas_call x1, Pallas kernels, local(): pl.pallas_call(functools.partial(kernel, peers, spans, rows, window), out...  61.6 us
    pallas_call x1, Pallas kernels, local(): pl.pallas_call(deliver, out_shape=shapes, in_specs=[loose] * 4, out_specs...  1.82 us

profile of v5, /device:TPU:1, one launch (start us, length us, event | category | flops | bytes accessed | tf_op | source)
XLA Modules:
  0.0 64.1 jit_solution(17311644217285247825)
XLA Ops:
  0.6 61.6 %shard_map.93 = (bf16[1,360,256]{2,1,0:T(8,128)(2,1)}, bf16[1,360,256]{2,1,0:T(8,128)(2,1)}, bf16[1,360,128]{2,1,0:T(8,128)(2,1)}, bf16[1,360,128]{2,1,0:T(8,128)(2,1)}) custom-call(bf16[1,360,256]{2,1,0:T(8,128)(2,1)} %refs_0_.1, bf16[1,360,128]{2,1,0:T(8,128)(2,1)} %refs_1_.1, bf16[1,360,128]{2,1,0:T(8,128)(2,1)} %refs_2_.1, bf16[1,360,256]{2,1,0:T(8,128)(2,1)} %refs_3_.1, ...), custom_call_target="tpu_custom_call" | custom-call | tf_op jit(solution)/shard_map/pallas_call | solution.py:391
  62.2 1.8 %shard_map.94 = (bf16[1,360,256]{2,1,0:T(8,128)(2,1)}, bf16[1,360,256]{2,1,0:T(8,128)(2,1)}, bf16[1,360,128]{2,1,0:T(8,128)(2,1)}, bf16[1,360,128]{2,1,0:T(8,128)(2,1)}) custom-call(bf16[1,360,256]{2,1,0:T(8,128)(2,1)} %get-tuple-element.8.refs_0_, bf16[1,360,256]{2,1,0:T(8,128)(2,1)} %get-tuple-element.9.refs_1_, ...), custom_call_target="tpu_custom_call" | custom-call | tf_op jit(solution)/shard_map/pallas_call | solution.py:428

commit v6 on v5

--- a/solution.py
+++ b/solution.py
@@ -210,6 +210,28 @@
         for back in range(spans):
             block = pl.ds(back * padded, padded)
             ctxt[half[side], block] = ctx[block, half[side]].astype(F32).T.astype(BF16)
+
+    def give(back, side):
+        near = back < spans - 1
+        sem = (2 * side + 1) * spans + back
+        return pltpu.make_async_remote_copy(
+            src_ref=gsend.at[back, :, half[side]],
+            dst_ref=grecv.at[back, :, half[side]],
+            send_sem=xssem.at[sem],
+            recv_sem=xrsem.at[sem],
+            device_id={"seq": lax.rem(shard + spans - (1 if near else back), spans)},
+            device_id_type=MESH,
+        )
+
+    def give_on(back, side):
+        @pl.when(shard >= back)
+        def _():
+            give(back, side).start()
+
+    def gets(back):
+        if back < spans - 1:
+            return (shard + 1 < spans) & (shard + 1 >= back)
+        return shard + back < spans
 
     def attend(member):
         if member == 0:
@@ -249,21 +271,31 @@
         if member == 0:
             exchange(3, *returning[3])
         center = center * share
-        dquery = jnp.zeros((HEAD, padded), F32)
-        for back in range(spans):
+        def keep(back, block, side, part):
+            if member == 0:
+                acc[block, half[side]] = part
+            else:
+                part = acc[block, half[side]] + part
+                gsend[back, :, half[side]] = part.astype(BF16)
+
+        def send_on(side):
+            if member == 1:
+                give_on(2, side)
+                give_on(spans - 1, side)
+
+        for back in range(spans - 1, -1, -1):
             block = pl.ds(back * padded, padded)
             prob = sbuf[block, :] * share
-            dscore = (prob * (dbuf[block, :] - center)).astype(BF16)
+            sbuf[block, :] = prob
+            keep(back, block, 1, dot(prob.astype(BF16), grad))
+        send_on(1)
+        dquery = jnp.zeros((HEAD, padded), F32)
+        for back in range(spans - 1, -1, -1):
+            block = pl.ds(back * padded, padded)
+            dscore = (sbuf[block, :] * (dbuf[block, :] - center)).astype(BF16)
             dquery = dquery + dot(ctxt[pl.ds(0, HEAD), block], dscore)
-            for at, part in (
-                (0, dot(dscore, query) * SCALE),
-                (HEAD, dot(prob.astype(BF16), grad)),
-            ):
-                if member == 0:
-                    acc[block, pl.ds(at, HEAD)] = part
-                else:
-                    part = acc[block, pl.ds(at, HEAD)] + part
-                    gsend[back, :, pl.ds(at, HEAD)] = part.astype(BF16)
+            keep(back, block, 0, dot(dscore, query) * SCALE)
+        send_on(0)
         homes[member, :, pl.ds(HEAD, HEAD)] = (dquery * SCALE).T.astype(BF16)
         if member == 0:
             exchange(7, *returning[7])
@@ -271,31 +303,6 @@
     attend(0)
     attend(1)
 
-    def give(back, side):
-        near = back < spans - 1
-        sem = (2 * side + 1) * spans + back
-        return pltpu.make_async_remote_copy(
-            src_ref=gsend.at[back, :, half[side]],
-            dst_ref=grecv.at[back, :, half[side]],
-            send_sem=xssem.at[sem],
-            recv_sem=xrsem.at[sem],
-            device_id={"seq": lax.rem(shard + spans - (1 if near else back), spans)},
-            device_id_type=MESH,
-        )
-
-    def give_on(back, side):
-        @pl.when(shard >= back)
-        def _():
-            give(back, side).start()
-
-    def gets(back):
-        if back < spans - 1:
-            return (shard + 1 < spans) & (shard + 1 >= back)
-        return shard + back < spans
-
-    for side in (1, 0):
-        give_on(2, side)
-        give_on(spans - 1, side)
     marks = (0, MIDDLE, 2 * MIDDLE, peers - 1)
     exchange(4, *returning[4], marks[0], marks[1])
     for side in (1, 0):

time: 64.3 us -> 63.7 us (level)
  no operation moved by 1% of the time
where the time goes in v6:
time: 63.7 us; the launch traced here: 63.5 us
  Pallas kernels  62.8 us (99%)
  between operations  0.64 us (1%)
    pallas_call x1, Pallas kernels, local(): pl.pallas_call(functools.partial(kernel, peers, spans, rows, window), out...  61 us
    pallas_call x1, Pallas kernels, local(): pl.pallas_call(deliver, out_shape=shapes, in_specs=[loose] * 4, out_specs...  1.82 us

profile of v6, /device:TPU:1, one launch (start us, length us, event | category | flops | bytes accessed | tf_op | source)
XLA Modules:
  0.0 63.5 jit_solution(6285342148828965514)
XLA Ops:
  0.6 61.0 %shard_map.93 = (bf16[1,360,256]{2,1,0:T(8,128)(2,1)}, bf16[1,360,256]{2,1,0:T(8,128)(2,1)}, bf16[1,360,128]{2,1,0:T(8,128)(2,1)}, bf16[1,360,128]{2,1,0:T(8,128)(2,1)}) custom-call(bf16[1,360,256]{2,1,0:T(8,128)(2,1)} %refs_0_.1, bf16[1,360,128]{2,1,0:T(8,128)(2,1)} %refs_1_.1, bf16[1,360,128]{2,1,0:T(8,128)(2,1)} %refs_2_.1, bf16[1,360,256]{2,1,0:T(8,128)(2,1)} %refs_3_.1, ...), custom_call_target="tpu_custom_call" | custom-call | tf_op jit(solution)/shard_map/pallas_call | solution.py:398
  61.7 1.8 %shard_map.94 = (bf16[1,360,256]{2,1,0:T(8,128)(2,1)}, bf16[1,360,256]{2,1,0:T(8,128)(2,1)}, bf16[1,360,128]{2,1,0:T(8,128)(2,1)}, bf16[1,360,128]{2,1,0:T(8,128)(2,1)}) custom-call(bf16[1,360,256]{2,1,0:T(8,128)(2,1)} %get-tuple-element.8.refs_0_, bf16[1,360,256]{2,1,0:T(8,128)(2,1)} %get-tuple-element.9.refs_1_, ...), custom_call_target="tpu_custom_call" | custom-call | tf_op jit(solution)/shard_map/pallas_call | solution.py:435
